TPU v7x, 32 devices: a whole 2x2x4 slice. The times are simulated.
32 devices in a mesh: dp: 8 (over z, core), seq: 4 (over y, x).
Axes of the slice: x: 2, y: 2, z: 4, core: 2. Of those that a mesh axis runs over, the one named last changes fastest.
Arguments:
- features: bfloat16 [16384, 1536], P(('dp', 'seq')), parts along dimension 0, may hold values from -6 to 6
- conv_taps: float32 [5, 1536], replicated, may hold values from -2.5 to 2.5
- norm_gain: float32 [1536], replicated, may hold values from 0.5 to 2
- point_weight: bfloat16 [1536, 1536], replicated, may hold values from -0.15625 to 0.15625
- donor_weight: bfloat16 [1536, 768], replicated, may hold values from -0.15625 to 0.15625
- accept_weight: bfloat16 [1536, 768], replicated, may hold values from -0.15625 to 0.15625
- donor_pos: int32 [2048], P(('dp', 'seq')), parts along dimension 0, may hold values from 0 to 2047, as said below
- accept_pos: int32 [2048], P(('dp', 'seq')), parts along dimension 0, may hold values from 0 to 2047, as said below
- pair_counts: int32 [32], P(('dp', 'seq')), parts along dimension 0, may hold values from 1 to 64, 128 in all
Outputs:
- encoded: bfloat16 [16384, 1536], P(('dp', 'seq')), parts along dimension 0
- junction: bfloat16 [2048, 768], P(('dp', 'seq')), parts along dimension 0
There are 8 independent parts, one for each index of `dp`. A program takes and returns all parts, laid end to end along the dimension named above; an argument that names none is the same for every part. Nothing has to cross between parts.
Inputs may be any that keep to these rules, and one draw needn't show every extreme that they name: `pair_counts`: the live counts sum to 128 and the largest is exactly 64. `donor_pos`: among the 128 donor and acceptor positions of the slots s * 64 to s * 64 + 63, at most 64 lie in any one block of 512 positions r * 512 to r * 512 + 511, and exactly 64 lie in one such block. `accept_pos`: as for donor_pos, with the two lists counted together.
All inputs are finite; a program needn't handle non-finite values. No bound on the sum of `pair_counts` on one device may be relied on, other than what follows from the above.
Results may differ from a plain program's by a relative error of at most 0.0064.
Values may be sent and summed in bfloat16 or wider, within the bound.
No kernel may reach another device: no remote copies, remote signals or barrier semaphores. Data moves between devices by JAX's collectives and lax.ppermute only.
A program may use at most 128 MiB of HBM per device.

v0:
```python
import jax
import jax.numpy as jnp
from jax import lax
from jax.sharding import PartitionSpec as P


def padded_2(array, sides, width):
    for axis, dim in sides:
        size, length = (lax.axis_size(axis), array.shape[dim])
        up = [(i, (i + 1) % size) for i in range(size - 1)]
        down = [(j, i) for i, j in up]
        last = lax.slice_in_dim(array, length - width, length, axis=dim)
        leading = lax.slice_in_dim(array, 0, width, axis=dim)
        before = lax.ppermute(last, axis, up)
        after = lax.ppermute(leading, axis, down)
        array = jnp.concatenate([before, array, after], axis=dim)
    return array


def on_device(
    features,
    conv_taps,
    norm_gain,
    point_weight,
    donor_weight,
    accept_weight,
    donor_pos,
    accept_pos,
    pair_counts,
):
    rows = features.shape[0]
    slots = donor_pos.shape[0]
    padded = padded_2(features, (("seq", 0),), 2).astype(jnp.float32)
    conv = conv_taps[0][None, :] * padded[0:rows]
    for k in range(1, conv_taps.shape[0]):
        conv = conv + conv_taps[k][None, :] * padded[k : k + rows]
    scale = lax.rsqrt(jnp.mean(conv * conv, axis=-1, keepdims=True) + 1e-06)
    normed = (conv * scale * norm_gain[None, :]).astype(jnp.bfloat16)
    mixed = jnp.dot(normed, point_weight, preferred_element_type=jnp.float32)
    encoded = (features.astype(jnp.float32) + jax.nn.gelu(mixed, approximate=False)).astype(
        jnp.bfloat16
    )
    channels = encoded.shape[1]
    owners = lax.axis_size("seq")
    capacity = 2 * ((2 * slots + owners - 1) // owners)
    wanted = jnp.concatenate([donor_pos, accept_pos])
    owner_of = wanted // rows
    one_hot = (owner_of[:, None] == jnp.arange(owners, dtype=jnp.int32)[None, :]).astype(jnp.int32)
    rank = jnp.sum((jnp.cumsum(one_hot, axis=0) - one_hot) * one_hot, axis=1)
    flat_slot = owner_of * capacity + rank
    asking = (
        jnp.full((owners * capacity,), -1, jnp.int32).at[flat_slot].set(wanted - owner_of * rows)
    )
    received = lax.all_to_all(
        asking.reshape(owners, capacity), "seq", split_axis=0, concat_axis=0, tiled=True
    )
    valid = received >= 0
    taken = jnp.take(encoded, jnp.clip(received, 0, rows - 1).reshape(owners * capacity), axis=0)
    taken = jnp.where(valid.reshape(owners * capacity)[:, None], taken, jnp.zeros_like(taken))
    returned = lax.all_to_all(
        taken.reshape(owners, capacity, channels), "seq", split_axis=0, concat_axis=0, tiled=True
    )
    picked = jnp.take(returned.reshape(owners * capacity, channels), flat_slot, axis=0)
    donor_rows = picked[:slots]
    accept_rows = picked[slots:]
    live = jnp.arange(slots, dtype=jnp.int32) < pair_counts[0]
    left = jnp.dot(donor_rows, donor_weight, preferred_element_type=jnp.float32)
    right = jnp.dot(accept_rows, accept_weight, preferred_element_type=jnp.float32)
    junction = jnp.where(live[:, None], jax.nn.silu(left) * right, jnp.float32(0.0)).astype(
        jnp.bfloat16
    )
    return (encoded, junction)


def solution(mesh):
    placed = (
        P(("dp", "seq"), None),
        P(),
        P(),
        P(),
        P(),
        P(),
        P(("dp", "seq")),
        P(("dp", "seq")),
        P(("dp", "seq")),
    )
    return jax.shard_map(
        on_device,
        mesh=mesh,
        in_specs=placed,
        out_specs=(P(("dp", "seq"), None), P(("dp", "seq"), None)),
        check_vma=False,
    )
```

profile of v0, /device:TPU:0, one launch (start us, length us, event | category | flops | bytes accessed | tf_op | source)
XLA Modules:
  0.0 57.2 jit_solution(17469958493648420995)
XLA Ops:
  0.6 0.0 copy-start
  0.6 0.9 %fusion.29 = (bf16[2,1536]{1,0:T(2,128)(2,1)S(1)}, bf16[2,1536]{1,0:T(2,128)(2,1)S(1)}) fusion(bf16[512,1536]{1,0:T(8,128)(2,1)} %param.9), kind=kLoop, calls=%fused_computation.83 | loop fusion | bytes 24576 | tf_op jit(solution)/shard_map/slice | solution.py:12
  1.6 4.9 %collective-permute-start = (bf16[2,1536]{1,0:T(2,128)(2,1)S(1)}, bf16[2,1536]{1,0:T(2,128)(2,1)S(1)}, u32[]{:S(2)}, u32[]{:S(2)}) collective-permute-start(bf16[2,1536]{1,0:T(2,128)(2,1)S(1)} %get-tuple-element.11), channel_id=1, source_target_pairs={{0,1},{1,2},{2,3},{4,5},{5,6},{6,7},{8,9},{9,10},{10,11},{12,13},{... | collective-permute-start | bytes 18440 | tf_op jit(solution)/shard_map/ppermute | solution.py:14
  6.4 1.3 %collective-permute-start.1 = (bf16[2,1536]{1,0:T(2,128)(2,1)S(1)}, bf16[2,1536]{1,0:T(2,128)(2,1)S(1)}, u32[]{:S(2)}, u32[]{:S(2)}) collective-permute-start(bf16[2,1536]{1,0:T(2,128)(2,1)S(1)} %get-tuple-element.12), channel_id=1, source_target_pairs={{1,0},{2,1},{3,2},{5,4},{6,5},{7,6},{9,8},{10,9},{11,10},{13,12},{... | collective-permute-start | bytes 18440 | tf_op jit(solution)/shard_map/ppermute | solution.py:15
  7.7 0.8 %multiply_subtract_fusion = (s32[128]{0:T(128)S(1)}, s32[128]{0:T(128)S(1)}) fusion(s32[64]{0:T(128)} %param.16, s32[64]{0:T(128)} %param.15), kind=kLoop, calls=%fused_computation.78 | loop fusion | flops 2304 | bytes 1536 | tf_op jit(solution)/shard_map/sub | solution.py:52
  8.5 0.1 fusion.23
  8.6 0.2 reduce_window_sum.11
  8.8 0.2 select_reduce_fusion
  8.9 0.8 %fusion.24 = s32[128]{0:T(128)S(1)} fusion(s32[128]{0:T(128)S(1)} %select_reduce_fusion, s32[64,1]{0,1:T(1,128)} %bitcast.25, s32[64,1]{0,1:T(1,128)} %bitcast.26), kind=kLoop, calls=%fused_computation.74 | loop fusion | flops 2688 | bytes 1536 | tf_op jit(solution)/shard_map/jit(_take)/jit(_where)/select_n | solution.py:63
  9.7 1.0 %scatter_custom_fusion = s32[256]{0:T(256)S(1)} fusion(s32[128]{0:T(128)S(1)} %fusion.24, s32[128]{0:T(128)S(1)} %get-tuple-element.7, s32[]{:T(128)} %constant.120.clone.1), kind=kCustom, calls=%fused_computation.79 | custom fusion | bytes 1028 | tf_op jit(solution)/shard_map/scatter | solution.py:52
  10.7 0.7 %all_to_all.9 = s32[4,1,64]{2,1,0:T(1,128)} reshape(s32[256]{0:T(256)S(1)} %scatter_custom_fusion) | data formatting | bytes 2048 | tf_op jit(solution)/shard_map/all_to_all | solution.py:54
  11.4 4.9 %all-to-all-start = ((s32[4,1,64]{2,1,0:T(1,128)}), s32[4,1,64]{2,1,0:T(1,128)S(1)}, u32[]{:S(2)}, u32[]{:S(2)}) async-start(s32[4,1,64]{2,1,0:T(1,128)} %all_to_all.9), calls=%async_computation | async-start | bytes 4096 | tf_op jit(solution)/shard_map/all_to_all | solution.py:54
  16.2 1.1 %slice_reduce_fusion.4 = (f32[1536]{0:T(1024)S(1)}, f32[1536]{0:T(1024)S(1)}, f32[1536]{0:T(1024)S(1)}, f32[1536]{0:T(1024)S(1)}, f32[1536]{0:T(1024)S(1)}) fusion(f32[5,1536]{1,0:T(8,128)} %param.10), kind=kLoop, calls=%fused_computation.53 | loop fusion | bytes 61440 | tf_op jit(solution)/shard_map/slice | solution.py:34
  17.3 3.5 %all-to-all-done = s32[4,1,64]{2,1,0:T(1,128)S(1)} async-done(((s32[4,1,64]{2,1,0:T(1,128)}), s32[4,1,64]{2,1,0:T(1,128)S(1)}, u32[]{:S(2)}, u32[]{:S(2)}) %all-to-all-start) | async-done | bytes 1056 | tf_op jit(solution)/shard_map/all_to_all | solution.py:54
  20.8 0.1 min.18
  21.0 0.0 collective-permute-done
  21.0 0.0 collective-permute-done.1
  21.0 0.0 slice-start
  21.0 2.0 %maximum_convert_fusion = f32[516,1536]{1,0:T(8,128)S(1)} fusion(bf16[2,1536]{1,0:T(2,128)(2,1)S(1)} %collective-permute-done.1, bf16[512,1536]{1,0:T(8,128)(2,1)} %param.9, bf16[2,1536]{1,0:T(2,128)(2,1)S(1)} %collective-permute-done), kind=kLoop, calls=%fused_computation.34 | loop fusion | flops 4755456 | bytes 4755456 | tf_op jit(solution)/shard_map/convert_element_type | solution.py:33
  23.0 0.0 copy-start.1
  23.1 0.0 slice-start.1
  23.1 0.0 copy-start.3
  23.1 2.4 %multiply_reduce_fusion = (f32[512]{0:T(512)S(1)}, f32[512,1536]{1,0:T(8,128)S(1)}) fusion(f32[516,1536]{1,0:T(8,128)S(1)} %maximum_convert_fusion, f32[1536]{0:T(1024)S(1)} %get-tuple-element.5, f32[1536]{0:T(1024)S(1)} %get-tuple-element.6, f32[1536]{0:T(1024)S(1)} %get-tuple-element.3, f32[1536]{0:T(1024)S(1)} %get-tuple-element.4, ...), kind=kLoop, calls=%fused_computation.31 | loop fusion | flops 8650240 | bytes 18907136 | tf_op jit(solution)/shard_map/reduce_sum | solution.py:37
  25.5 0.0 slice-done
  25.5 0.0 copy-done.1
  25.6 0.0 slice-done.1
  25.6 0.0 copy-done.3
  25.6 10.6 %fusion.3 = bf16[512,1536]{1,0:T(8,128)(2,1)} fusion(bf16[512,1536]{1,0:T(8,128)(2,1)S(1)} %copy-done.1, bf16[1536,1536]{1,0:T(8,128)(2,1)S(1)} %bitcast.28, f32[512,1536]{1,0:T(8,128)S(1)} %get-tuple-element.10, f32[1536]{0:T(1024)S(1)} %copy-done.3, f32[512]{0:T(512)S(1)} %add_rsqrt_fusion), kind=kOutput, calls=%fused_computation.7 | convolution fusion | flops 2470969344 | bytes 11018240 | tf_op jit(solution)/shard_map/dot_general | solution.py:39
  36.2 3.6 %gather_fusion = bf16[256,1536]{1,0:T(8,128)(2,1)S(1)} fusion(bf16[512,1536]{1,0:T(8,128)(2,1)} %fusion.3, s32[1024]{0:T(1024)S(1)} %pad_clamp_fusion.1), kind=kCustom, calls=%fused_computation | custom fusion | bytes 1573888 | tf_op jit(solution)/shard_map/jit(_take)/gather | solution.py:58
  39.8 1.1 %select_select_fusion = bf16[4,64,1536]{2,1,0:T(8,128)(2,1)} fusion(bf16[4,64,1536]{2,1,0:T(8,128)(2,1)S(1)} %bitcast.21, pred[4,64]{1,0:T(4,128)(4,1)S(1)} %compare_and_fusion, pred[4,64]{1,0:T(4,128)(4,1)S(1)} %bitcast.24), kind=kLoop, calls=%fused_computation.41 | loop fusion | flops 786432 | bytes 1573376 | tf_op jit(solution)/shard_map/jit(_where)/select_n | solution.py:59
  40.9 3.5 %all-to-all-start.1 = ((bf16[4,64,1536]{2,1,0:T(8,128)(2,1)}), bf16[4,64,1536]{2,1,0:T(8,128)(2,1)S(1)}, u32[]{:S(2)}, u32[]{:S(2)}) async-start(bf16[4,64,1536]{2,1,0:T(8,128)(2,1)} %select_select_fusion), calls=%async_computation.1 | async-start | bytes 1572864 | tf_op jit(solution)/shard_map/all_to_all | solution.py:60
  45.1 8.4 %all-to-all-done.1 = bf16[4,64,1536]{2,1,0:T(8,128)(2,1)S(1)} async-done(((bf16[4,64,1536]{2,1,0:T(8,128)(2,1)}), bf16[4,64,1536]{2,1,0:T(8,128)(2,1)S(1)}, u32[]{:S(2)}, u32[]{:S(2)}) %all-to-all-start.1) | async-done | bytes 786464 | tf_op jit(solution)/shard_map/all_to_all | solution.py:60
  53.5 0.9 %gather_fusion.1 = bf16[128,1536]{1,0:T(8,128)(2,1)S(1)} fusion(bf16[256,1536]{1,0:T(8,128)(2,1)S(1)} %bitcast.20, s32[1024]{0:T(1024)S(1)} %pad_clamp_fusion), kind=kCustom, calls=%fused_computation.1 | custom fusion | bytes 786944 | tf_op jit(solution)/shard_map/jit(_take)/gather | solution.py:63
  54.4 0.0 copy-start.2
  54.4 0.1 broadcast_select_fusion
  54.5 0.0 copy-done
  54.5 0.5 fusion.21
  55.0 1.0 %copy-done.2 = bf16[1536,768]{1,0:T(8,128)(2,1)S(1)} copy-done((bf16[1536,768]{1,0:T(8,128)(2,1)S(1)}, bf16[1536,768]{1,0:T(8,128)(2,1)}, u32[]{:S(2)}) %copy-start.2) | copy-done | bytes 2359320
  56.1 1.2 %fusion.19 = bf16[64,768]{1,0:T(8,128)(2,1)} fusion(bf16[1536,768]{1,0:T(8,128)(2,1)S(1)} %copy-done.2, bf16[128,1536]{1,0:T(8,128)(2,1)S(1)} %broadcast_select_fusion, f32[64,768]{1,0:T(8,128)S(1)} %fusion.21, pred[64]{0:T(512)(128)(4,1)S(1)} %iota_compare_fusion.1), kind=kOutput, calls=%fused_computation.40 | convolution fusion | flops 151339008 | bytes 2851328 | tf_op jit(solution)/shard_map/dot_general | solution.py:68
  (11 shorter events, 0.1 us)
Async XLA Ops:
  0.6 53.9 %copy-start = (bf16[1536,768]{1,0:T(8,128)(2,1)S(1)}, bf16[1536,768]{1,0:T(8,128)(2,1)}, u32[]{:S(2)}) copy-start(bf16[1536,768]{1,0:T(8,128)(2,1)} %param.13) | copy-start | bytes 7077892
  1.6 19.4 %collective-permute-start = (bf16[2,1536]{1,0:T(2,128)(2,1)S(1)}, bf16[2,1536]{1,0:T(2,128)(2,1)S(1)}, u32[]{:S(2)}, u32[]{:S(2)}) collective-permute-start(bf16[2,1536]{1,0:T(2,128)(2,1)S(1)} %get-tuple-element.11), channel_id=1, source_target_pairs={{0,1},{1,2},{2,3},{4,5},{5,6},{6,7},{8,9},{9,10},{10,11},{12,13},{... | collective-permute-start | bytes 18440 | tf_op jit(solution)/shard_map/ppermute | solution.py:14
  6.4 14.5 %collective-permute-start.1 = (bf16[2,1536]{1,0:T(2,128)(2,1)S(1)}, bf16[2,1536]{1,0:T(2,128)(2,1)S(1)}, u32[]{:S(2)}, u32[]{:S(2)}) collective-permute-start(bf16[2,1536]{1,0:T(2,128)(2,1)S(1)} %get-tuple-element.12), channel_id=1, source_target_pairs={{1,0},{2,1},{3,2},{5,4},{6,5},{7,6},{9,8},{10,9},{11,10},{13,12},{... | collective-permute-start | bytes 18440 | tf_op jit(solution)/shard_map/ppermute | solution.py:15
  11.4 9.5 %all-to-all-start = ((s32[4,1,64]{2,1,0:T(1,128)}), s32[4,1,64]{2,1,0:T(1,128)S(1)}, u32[]{:S(2)}, u32[]{:S(2)}) async-start(s32[4,1,64]{2,1,0:T(1,128)} %all_to_all.9), calls=%async_computation | async-start | bytes 4096 | tf_op jit(solution)/shard_map/all_to_all | solution.py:54
  21.0 4.5 %slice-start = ((s8[4718592]{0:T(1024)(128)(4,1)}), s8[4194304]{0:T(1024)(128)(4,1)S(1)}, s32[]{:S(2)}) async-start(s8[4718592]{0:T(1024)(128)(4,1)} %bitcast.27), calls=%async_computation.2 | async-start | bytes 8388608
  23.0 2.5 %copy-start.1 = (bf16[512,1536]{1,0:T(8,128)(2,1)S(1)}, bf16[512,1536]{1,0:T(8,128)(2,1)}, u32[]{:S(2)}) copy-start(bf16[512,1536]{1,0:T(8,128)(2,1)} %param.9) | copy-start | bytes 4718596
  23.1 2.5 %slice-start.1 = ((s8[4718592]{0:T(1024)(128)(4,1)}), s8[524288]{0:T(1024)(128)(4,1)S(1)}, s32[]{:S(2)}) async-start(s8[4718592]{0:T(1024)(128)(4,1)} %bitcast.27), calls=%async_computation.3 | async-start | bytes 1048576
  23.1 2.5 %copy-start.3 = (f32[1536]{0:T(1024)S(1)}, f32[1536]{0:T(1024)}, u32[]{:S(2)}) copy-start(f32[1536]{0:T(1024)} %param.11) | copy-start | bytes 18436
  40.9 12.6 %all-to-all-start.1 = ((bf16[4,64,1536]{2,1,0:T(8,128)(2,1)}), bf16[4,64,1536]{2,1,0:T(8,128)(2,1)S(1)}, u32[]{:S(2)}, u32[]{:S(2)}) async-start(bf16[4,64,1536]{2,1,0:T(8,128)(2,1)} %select_select_fusion), calls=%async_computation.1 | async-start | bytes 1572864 | tf_op jit(solution)/shard_map/all_to_all | solution.py:60
  54.4 1.7 %copy-start.2 = (bf16[1536,768]{1,0:T(8,128)(2,1)S(1)}, bf16[1536,768]{1,0:T(8,128)(2,1)}, u32[]{:S(2)}) copy-start(bf16[1536,768]{1,0:T(8,128)(2,1)} %param.14) | copy-start | bytes 7077892
where the time goes:
time: 57.7 us; the launch traced here: 57.2 us
  starting transfers between devices  14.5 us (25%)
  matrix products  12.3 us (21%)
  waiting for transfers between devices  11.9 us (21%)
  local copies, waits for them, and re-layouts  9.29 us (16%)
  other arithmetic  7.63 us (13%)
  between operations  1.53 us (3%)
    dot_general x1, matrix products, on_device(): mixed = jnp.dot(normed, point_weight, preferred_element_type=jnp.float32)  10.6 us
    all_to_all x1, waiting for transfers between devices, on_device(): lax.all_to_all(taken.reshape(owners, capacity, channels), 'seq', split_ax...  8.44 us
    ppermute x1, starting transfers between devices, padded_2(): before = lax.ppermute(last, axis, up)  4.87 us
    all_to_all x1, starting transfers between devices, on_device(): lax.all_to_all(asking.reshape(owners, capacity), 'seq', split_axis=0, con...  4.87 us
    gather x1, local copies, waits for them, and re-layouts, on_device(): jnp.take(encoded, jnp.clip(received, 0, rows - 1).reshape(owners * capaci...  3.6 us
    all_to_all x1, waiting for transfers between devices, on_device(): lax.all_to_all(asking.reshape(owners, capacity), 'seq', split_axis=0, con...  3.5 us
    all_to_all x1, starting transfers between devices, on_device(): lax.all_to_all(taken.reshape(owners, capacity, channels), 'seq', split_ax...  3.49 us
    reduce_sum x1, other arithmetic, on_device(): scale = lax.rsqrt(jnp.mean(conv * conv, axis=-1, keepdims=True) + 1e-06)  2.43 us
  transfers between devices with their start and end apart: 4, of which 2 were waited for; matrix products, arithmetic and copies ran while one was open for 7% of the time, Pallas kernels for 0%

commit v1 on v0

v1 whole, which is shorter than its diff:
```python
import functools

import jax
import jax.numpy as jnp
from jax import lax
from jax.experimental import pallas as pl
from jax.experimental.pallas import tpu as pltpu
from jax.sharding import PartitionSpec as P

F32 = jnp.float32
BF16 = jnp.bfloat16
LANES = 128
HALO = 2
MIB = 1 << 20


def vmem(shape, dtype):
    return pltpu.VMEM(shape, dtype)


def whole():
    return pl.BlockSpec(memory_space=pltpu.VMEM)


def far(array):
    return pltpu.with_memory_space_constraint(array, pltpu.MemorySpace.HBM)


def in_hbm():
    return pl.BlockSpec(memory_space=pltpu.MemorySpace.HBM)


def params(mib):
    return pltpu.CompilerParams(vmem_limit_bytes=mib * MIB)


def gelu(v):
    m = jnp.abs(v)
    d = m * F32(0.3275911 * 0.7071067811865476) + F32(1.0)
    u = pl.reciprocal(d, approx=False)
    p = u * F32(0.5 * 1.061405429) + F32(0.5 * -1.453152027)
    p = p * u + F32(0.5 * 1.421413741)
    p = p * u + F32(0.5 * -0.284496736)
    p = p * u + F32(0.5 * 0.254829592)
    e = jnp.exp2(v * v * F32(-0.5 * 1.4426950408889634))
    return jnp.maximum(v, F32(0.0)) - (m * u) * (p * e)


def pack_kernel(feat_hbm, donor_hbm, accept_hbm, count, out_ref, ends, donor, accept, sem):
    channels = out_ref.shape[1]
    rows = feat_hbm.shape[0]
    loads = [
        pltpu.make_async_copy(feat_hbm.at[pl.ds(0, 8)], ends.at[0], sem.at[0]),
        pltpu.make_async_copy(feat_hbm.at[pl.ds(rows - 8, 8)], ends.at[1], sem.at[1]),
        pltpu.make_async_copy(donor_hbm, donor, sem.at[2]),
        pltpu.make_async_copy(accept_hbm, accept, sem.at[3]),
    ]
    for load in loads:
        load.start()
    for load in loads:
        load.wait()
    first = ends[0].astype(F32)
    last = pltpu.roll(ends[1].astype(F32), 2 * HALO, axis=0)
    row = lax.broadcasted_iota(jnp.int32, (8, channels), 0)
    rows = jnp.where(row < HALO, first, jnp.where(row < 2 * HALO, last, F32(0.0)))
    wanted = jnp.concatenate([donor[...], accept[...]], axis=1)
    width = wanted.shape[1]
    live = jnp.full((1, width), count[0], jnp.int32)
    line = jnp.concatenate([wanted >> 8, wanted & 255, live], axis=1).astype(F32)
    spot = lax.broadcasted_iota(jnp.int32, (8, 3 * width), 0) == 2 * HALO
    out_ref[:, 0 : 3 * width] = jnp.where(spot, line, rows[:, 0 : 3 * width]).astype(BF16)
    out_ref[:, 3 * width :] = rows[:, 3 * width :].astype(BF16)


def pack(features, donor, accept, count):
    rows, channels = features.shape
    slots = donor.shape[0]
    return pl.pallas_call(
        pack_kernel,
        in_specs=[in_hbm()] * 3 + [pl.BlockSpec(memory_space=pltpu.SMEM)],
        out_specs=whole(),
        out_shape=vmem((8, channels), BF16),
        scratch_shapes=[
            pltpu.VMEM((2, 8, channels), BF16),
            pltpu.VMEM((1, slots), jnp.int32),
            pltpu.VMEM((1, slots), jnp.int32),
            pltpu.SemaphoreType.DMA((4,)),
        ],
        compiler_params=params(4),
        name="pack",
    )(far(features), far(donor.reshape(1, slots)), far(accept.reshape(1, slots)), count)


def unpack_line(packet_ref, width):
    line = packet_ref[...].astype(F32)[2 * HALO : 2 * HALO + 1, 0 : 3 * width]
    wanted = line[:, 0:width] * F32(256.0) + line[:, width : 2 * width]
    lane = lax.broadcasted_iota(jnp.int32, (1, width), 1)
    slot = jnp.where(lane >= width // 2, lane - width // 2, lane).astype(F32)
    return wanted, slot < line[:, 2 * width :]


def strict_upper(size):
    a = lax.broadcasted_iota(jnp.int32, (size, size), 0)
    b = lax.broadcasted_iota(jnp.int32, (size, size), 1)
    return (a < b).astype(F32).astype(BF16)


def chosen(mine, capacity):
    ranks = jnp.dot(mine.astype(BF16), strict_upper(mine.shape[1]), preferred_element_type=F32)
    keyed = jnp.where(mine > F32(0.5), ranks, F32(-1.0))
    level = lax.broadcasted_iota(jnp.int32, (capacity, mine.shape[1]), 0).astype(F32)
    return lambda k: keyed[k : k + 1, :] == level


def conv_rows(load, taps_ref, gain_ref, columns, eps_scale):
    tap_count = taps_ref.shape[0]
    held = []
    total = None
    for j in range(columns):
        lanes = slice(j * LANES, (j + 1) * LANES)
        acc = None
        for k in range(tap_count):
            term = taps_ref[k : k + 1, lanes] * load(j, k)
            acc = term if acc is None else acc + term
        held.append(acc)
        total = acc * acc if total is None else total + acc * acc
    mean = jnp.sum(total, axis=-1, keepdims=True) * F32(eps_scale)
    scale = lax.rsqrt(mean + F32(1e-06))
    return [
        (held[j] * scale * gain_ref[0:1, j * LANES : (j + 1) * LANES]).astype(BF16)
        for j in range(columns)
    ]


def conv_kernel(
    owners,
    capacity,
    width,
    packet_ref,
    feat_hbm,
    taps_ref,
    gain_ref,
    w_hbm,
    normed_ref,
    feat_ref,
    w_ref,
    spread_ref,
    wide,
    feat_sem,
    weight_sem,
):
    rows, channels = feat_ref.shape
    columns = channels // LANES
    parts = 4
    step = rows // parts
    loads = [
        pltpu.make_async_copy(
            feat_hbm.at[pl.ds(c * step, step)], feat_ref.at[pl.ds(c * step, step)], feat_sem.at[c]
        )
        for c in range(parts)
    ]
    for load in loads:
        load.start()
    weights = [pltpu.make_async_copy(w_hbm, w_ref, weight_sem.at[0])]
    for load in weights:
        load.start()

    me = lax.axis_index("seq")
    wanted, live = unpack_line(packet_ref, width)
    group = lax.broadcasted_iota(jnp.int32, (max(8, owners), width), 0)
    low = ((group ^ me) * rows).astype(F32)
    here = (wanted >= low) & (wanted < low + F32(rows)) & live & (group < owners)
    pick = chosen(jnp.where(here, F32(1.0), F32(0.0)), capacity)
    for k in range(owners):
        spread_ref[k * capacity : (k + 1) * capacity, :] = jnp.where(
            pick(k), F32(1.0), F32(0.0)
        ).astype(BF16)

    edge = jnp.zeros((8, LANES), F32)
    for j in range(columns):
        wide[j, 0:8, :] = edge
        wide[j, rows + 8 : rows + 16, :] = edge

    tile = 32

    def widen(c):
        loads[c].wait()
        for j in range(columns):
            lanes = slice(j * LANES, (j + 1) * LANES)
            wide[j, 8 + c * step : 8 + (c + 1) * step, :] = feat_ref[
                c * step : (c + 1) * step, lanes
            ].astype(F32)

    def convolve(first, count):
        def body(i, carry):
            base = pl.multiple_of(first + i * tile, tile)

            def load(j, k):
                return wide.at[j, pl.ds(base, tile + 16), :][8 - HALO + k : 8 - HALO + k + tile, :]

            out = conv_rows(load, taps_ref, gain_ref, columns, 1.0 / channels)
            for j in range(columns):
                normed_ref[pl.ds(base, tile), j * LANES : (j + 1) * LANES] = out[j]
            return carry

        lax.fori_loop(0, count, body, 0)

    widen(0)
    done = 0
    for c in range(1, parts):
        widen(c)
        ready = c * step // tile * tile
        convolve(done, (ready - done) // tile)
        done = ready
    convolve(done, (rows - done) // tile)
    for load in weights:
        load.wait()


def conv_norm(packet, features, taps, gain, w, owners, capacity, width):
    rows, channels = features.shape
    return pl.pallas_call(
        functools.partial(conv_kernel, owners, capacity, width),
        in_specs=[whole(), in_hbm(), whole(), whole(), in_hbm()],
        out_specs=[whole()] * 4,
        out_shape=[
            vmem((rows, channels), BF16),
            vmem((rows, channels), BF16),
            vmem(w.shape, BF16),
            vmem((owners * capacity, width), BF16),
        ],
        scratch_shapes=[
            pltpu.VMEM((channels // LANES, rows + 16, LANES), F32),
            pltpu.SemaphoreType.DMA((4,)),
            pltpu.SemaphoreType.DMA((1,)),
        ],
        compiler_params=params(6),
        cost_estimate=pl.CostEstimate(flops=30 * rows * channels, bytes_accessed=12 << 20, transcendentals=rows),
        name="conv_norm",
    )(packet, far(features), taps, gain.reshape(1, channels), far(w))


def named_kernel(owners, capacity, width, *refs):
    packets = refs[:owners]
    feat_ref, normed_ref, taps_ref, gain_ref, w_ref, wd_hbm, wa_hbm = refs[owners : owners + 7]
    outs = refs[owners + 7 : 2 * owners + 7]
    patched_ref = refs[2 * owners + 7]
    near, grab, lhs, res, enc, wd_ref, wa_ref, sem = refs[2 * owners + 8 :]
    del normed_ref
    weights = [
        pltpu.make_async_copy(wd_hbm, wd_ref, sem.at[0]),
        pltpu.make_async_copy(wa_hbm, wa_ref, sem.at[1]),
    ]
    for load in weights:
        load.start()
    rows, channels = feat_ref.shape
    columns = channels // LANES
    heads = wd_ref.shape[1]
    me = lax.axis_index("seq")

    above = jnp.zeros((8, channels), F32)
    below = jnp.zeros((8, channels), F32)
    for k in range(1, owners):
        other = packets[k][...].astype(F32)
        above = jnp.where((me ^ k) == me - 1, other, above)
        below = jnp.where((me ^ k) == me + 1, other, below)
    row = lax.broadcasted_iota(jnp.int32, (8, channels), 0)
    above = jnp.where(row >= 8 - HALO, pltpu.roll(above, 8 - 2 * HALO, axis=0), F32(0.0))
    below = jnp.where(row < HALO, below, F32(0.0))
    span = 16
    head = feat_ref[0 : span + 8, :].astype(F32)
    foot = feat_ref[rows - span - 8 : rows, :].astype(F32)
    for j in range(columns):
        lanes = slice(j * LANES, (j + 1) * LANES)
        near[j, 0:8, :] = above[:, lanes]
        near[j, 8 : 16 + span, :] = head[:, lanes]
        near[j, 16 + span : 24 + 2 * span, :] = foot[:, lanes]
        near[j, 24 + 2 * span : 32 + 2 * span, :] = below[:, lanes]
    for origin, place in ((8, 0), (24 + span, rows - span)):

        def load(j, k, origin=origin):
            begin = origin - HALO + k
            return near[j, begin : begin + span, :]

        out = conv_rows(load, taps_ref, gain_ref, columns, 1.0 / channels)
        for j in range(columns):
            patched_ref[place : place + span, j * LANES : (j + 1) * LANES] = out[j]

    groups = max(8, owners)
    group = lax.broadcasted_iota(jnp.int32, (groups, width), 0)
    lane = lax.broadcasted_iota(jnp.int32, (1, width), 1)
    local = jnp.zeros((groups, width), F32)
    mine = jnp.zeros((groups, width), F32)
    start = (me * rows).astype(F32)
    for k in range(owners):
        at, live = unpack_line(packets[k], width)
        at = at - start
        here = (at >= F32(0.0)) & (at < F32(rows)) & live
        mine = jnp.where(group == k, jnp.where(here, F32(1.0), F32(0.0)), mine)
        local = jnp.where(group == k, at, local)
    pick = chosen(mine, capacity)
    mark = F32(1 << 16)
    keyed = local + F32(1.0) + jnp.where(lane >= width // 2, mark, F32(0.0))
    spread = lax.broadcasted_iota(jnp.int32, (capacity, rows), 1).astype(F32)
    kinds = []
    for k in range(owners):
        code = jnp.sum(jnp.where(pick(k), keyed[k : k + 1, :], F32(0.0)), axis=1, keepdims=True)
        accepts = code >= mark
        kinds.append(accepts)
        index = code - jnp.where(accepts, mark, F32(0.0)) - F32(1.0)
        grab[k * capacity : (k + 1) * capacity, :] = jnp.where(
            spread == index, F32(1.0), F32(0.0)
        ).astype(BF16)

    wide = 256
    for j in range(channels // wide):
        lanes = slice(j * wide, (j + 1) * wide)
        lhs[:, lanes] = jnp.dot(
            grab[...], patched_ref[:, lanes], preferred_element_type=F32
        ).astype(BF16)
        res[:, lanes] = jnp.dot(
            grab[...], feat_ref[:, lanes], preferred_element_type=F32
        ).astype(BF16)
    for j in range(channels // wide):
        lanes = slice(j * wide, (j + 1) * wide)
        mixed = jnp.dot(lhs[...], w_ref[:, lanes], preferred_element_type=F32)
        enc[:, lanes] = (res[:, lanes].astype(F32) + gelu(mixed)).astype(BF16)
    for load in weights:
        load.wait()
    for j in range(heads // wide):
        lanes = slice(j * wide, (j + 1) * wide)
        left = jnp.dot(enc[...], wd_ref[:, lanes], preferred_element_type=F32)
        right = jnp.dot(enc[...], wa_ref[:, lanes], preferred_element_type=F32)
        for k in range(owners):
            part = slice(k * capacity, (k + 1) * capacity)
            outs[k][:, lanes] = jnp.where(kinds[k], right[part], left[part]).astype(BF16)


def named(packets, feat, normed, taps, gain, w, wd, wa, width, capacity):
    owners = len(packets)
    rows, channels = feat.shape
    heads = wd.shape[1]
    total = owners * capacity
    out = pl.pallas_call(
        functools.partial(named_kernel, owners, capacity, width),
        in_specs=[whole()] * (owners + 5) + [in_hbm()] * 2,
        out_specs=[whole()] * (owners + 1),
        out_shape=[vmem((capacity, heads), BF16)] * owners + [vmem((rows, channels), BF16)],
        input_output_aliases={owners + 1: owners},
        scratch_shapes=[
            pltpu.VMEM((channels // LANES, 64, LANES), F32),
            pltpu.VMEM((total, rows), BF16),
            pltpu.VMEM((total, channels), BF16),
            pltpu.VMEM((total, channels), BF16),
            pltpu.VMEM((total, channels), BF16),
            pltpu.VMEM(wd.shape, BF16),
            pltpu.VMEM(wa.shape, BF16),
            pltpu.SemaphoreType.DMA((2,)),
        ],
        compiler_params=params(16),
        cost_estimate=pl.CostEstimate(
            flops=4 * total * channels * (channels + rows), bytes_accessed=8 << 20, transcendentals=2 * total * channels
        ),
        name="named_rows",
    )(*packets, feat, normed, taps, gain.reshape(1, channels), w, far(wd), far(wa))
    return out[:owners], out[owners]


def encode_kernel(normed_ref, feat_ref, w_ref, out_hbm, stage, sem):
    rows, channels = feat_ref.shape
    wide = 256
    tall = 256
    copies = []
    for j in range(channels // wide):
        lanes = slice(j * wide, (j + 1) * wide)
        for i in range(rows // tall):
            part = slice(i * tall, (i + 1) * tall)
            mixed = jnp.dot(normed_ref[part, :], w_ref[:, lanes], preferred_element_type=F32)
            stage[part, lanes] = (feat_ref[part, lanes].astype(F32) + gelu(mixed)).astype(BF16)
        copy = pltpu.make_async_copy(
            stage.at[:, pl.ds(j * wide, wide)], out_hbm.at[:, pl.ds(j * wide, wide)], sem.at[j]
        )
        copy.start()
        copies.append(copy)
    for copy in copies:
        copy.wait()


def encode(normed, feat, w):
    rows, channels = feat.shape
    return pl.pallas_call(
        encode_kernel,
        in_specs=[whole()] * 3,
        out_specs=pl.BlockSpec(memory_space=pltpu.MemorySpace.HBM),
        out_shape=jax.ShapeDtypeStruct((rows, channels), BF16),
        scratch_shapes=[pltpu.VMEM((rows, channels), BF16), pltpu.SemaphoreType.DMA((channels // 256,))],
        compiler_params=params(6),
        cost_estimate=pl.CostEstimate(
            flops=2 * rows * channels * channels, bytes_accessed=8 << 20, transcendentals=2 * rows * channels
        ),
        name="encode",
    )(normed, feat, w)


def junction_kernel(owners, *refs):
    blocks = refs[:owners]
    spread_ref, out_ref = refs[owners:]
    slots = out_ref.shape[0]
    capacity = blocks[0].shape[0]
    picked = None
    for k in range(owners):
        part = lax.dot_general(
            spread_ref[k * capacity : (k + 1) * capacity, :],
            blocks[k][...],
            (((0,), (0,)), ((), ())),
            preferred_element_type=F32,
        )
        picked = part if picked is None else picked + part
    left, right = picked[:slots], picked[slots:]
    silu = left / (F32(1.0) + jnp.exp(-left))
    out_ref[...] = (silu * right).astype(BF16)


def junction(blocks, spread):
    slots = spread.shape[1] // 2
    heads = blocks[0].shape[1]
    return pl.pallas_call(
        functools.partial(junction_kernel, len(blocks)),
        in_specs=[whole()] * (len(blocks) + 1),
        out_specs=whole(),
        out_shape=jax.ShapeDtypeStruct((slots, heads), BF16),
        compiler_params=params(6),
        name="junction",
    )(*blocks, spread)


def swap(array, k, owners):
    return lax.ppermute(array, "seq", [(i, i ^ k) for i in range(owners)])


def on_device(
    features,
    conv_taps,
    norm_gain,
    point_weight,
    donor_weight,
    accept_weight,
    donor_pos,
    accept_pos,
    pair_counts,
):
    slots = donor_pos.shape[0]
    owners = lax.axis_size("seq")
    capacity = 2 * ((2 * slots + owners - 1) // owners)
    own = pack(features, donor_pos, accept_pos, pair_counts)
    packets = [own] + [swap(own, k, owners) for k in range(1, owners)]
    width = 2 * slots
    normed, feat, w, spread = conv_norm(
        own, features, conv_taps, norm_gain, point_weight, owners, capacity, width
    )
    sends, patched = named(
        packets, feat, normed, conv_taps, norm_gain, w, donor_weight, accept_weight, width, capacity
    )
    blocks = [sends[0]] + [swap(sends[k], k, owners) for k in range(1, owners)]
    encoded = encode(patched, feat, w)
    return encoded, junction(blocks, spread)


def solution(mesh):
    placed = (
        P(("dp", "seq"), None),
        P(),
        P(),
        P(),
        P(),
        P(),
        P(("dp", "seq")),
        P(("dp", "seq")),
        P(("dp", "seq")),
    )
    return jax.shard_map(
        on_device,
        mesh=mesh,
        in_specs=placed,
        out_specs=(P(("dp", "seq"), None), P(("dp", "seq"), None)),
        check_vma=False,
    )
```

time: 57.7 us -> 28 us (0.49)
  Pallas kernels: 0 us -> 17.8 us
  matrix products: 12.3 us -> 0 us
  waiting for transfers between devices: 11.9 us -> 0.34 us
  local copies, waits for them, and re-layouts: 9.29 us -> 0.01 us
  other arithmetic: 7.63 us -> 0 us
  starting transfers between devices: 14.5 us -> 8.18 us
    pallas_call x0 -> x5, Pallas kernels: none -> 17.8 us  [the longest x1 6.59 us: named(): pl.pallas_call(functools.partial(named_kernel, owners, capacity, width),...]
    dot_general x3 -> x0, matrix products: 12.3 us -> none  [the longest x1 10.6 us: on_device(): mixed = jnp.dot(normed, point_weight, preferred_element_type=jnp.float32)]
    all_to_all x2 -> x0, waiting for transfers between devices: 11.9 us -> none  [the longest x1 8.44 us: on_device(): lax.all_to_all(taken.reshape(owners, capacity, channels), 'seq', split_ax...]
    all_to_all x2 -> x0, starting transfers between devices: 8.36 us -> none  [the longest x1 4.87 us: on_device(): lax.all_to_all(asking.reshape(owners, capacity), 'seq', split_axis=0, con...]
    gather x2 -> x0, local copies, waits for them, and re-layouts: 4.5 us -> none  [the longest x1 3.6 us: on_device(): jnp.take(encoded, jnp.clip(received, 0, rows - 1).reshape(owners * capaci...]
    reduce_sum x2 -> x0, other arithmetic: 2.61 us -> none  [the longest x1 2.43 us: on_device(): scale = lax.rsqrt(jnp.mean(conv * conv, axis=-1, keepdims=True) + 1e-06)]
    convert_element_type x2 -> x0, other arithmetic: 2.1 us -> none  [the longest x1 2.02 us: on_device(): padded = padded_2(features, (('seq', 0),), 2).astype(jnp.float32)]
    ppermute x2 -> x6, starting transfers between devices: 6.16 us -> 8.18 us  [swap(): return lax.ppermute(array, 'seq', [(i, i ^ k) for i in range(owners)])]
  transfers between devices with their start and end apart: 4 -> 6, of which waited for: 2 -> 1; matrix products, arithmetic and copies ran while one was open for 7% -> 0% of each run, Pallas kernels for 0% -> 34%
where the time goes in v1:
time: 28 us; the launch traced here: 27.7 us
  Pallas kernels  17.8 us (64%)
  starting transfers between devices  8.18 us (29%)
  between operations  1.39 us (5%)
  waiting for transfers between devices  0.34 us (1%)
    ppermute x6, starting transfers between devices, swap(): return lax.ppermute(array, 'seq', [(i, i ^ k) for i in range(owners)])  8.18 us
    pallas_call x1, Pallas kernels, named(): pl.pallas_call(functools.partial(named_kernel, owners, capacity, width),...  6.59 us
    pallas_call x1, Pallas kernels, encode(): pl.pallas_call(encode_kernel, in_specs=[whole()] * 3, out_specs=pl.BlockS...  5.08 us
    pallas_call x1, Pallas kernels, conv_norm(): pl.pallas_call(functools.partial(conv_kernel, owners, capacity, width), i...  4.21 us
    pallas_call x1, Pallas kernels, junction(): pl.pallas_call(functools.partial(junction_kernel, len(blocks)), in_specs=...  1.05 us
    pallas_call x1, Pallas kernels, pack(): pl.pallas_call(pack_kernel, in_specs=[in_hbm()] * 3 + [pl.BlockSpec(memor...  0.87 us
  transfers between devices with their start and end apart: 6, of which 1 were waited for; matrix products, arithmetic and copies ran while one was open for 0% of the time, Pallas kernels for 34%

profile of v1, /device:TPU:0, one launch (start us, length us, event | category | flops | bytes accessed | tf_op | source)
XLA Modules:
  0.0 27.7 jit_solution(11499655252855396652)
XLA Ops:
  0.6 0.0 copy-start.1
  0.6 0.0 copy-start
  1.3 0.9 %pack.1.packet_ref.refs_0_ = bf16[8,1536]{1,0:T(8,128)(2,1)S(1)} custom-call(bf16[512,1536]{1,0:T(8,128)(2,1)} %feat_hbm.3, s32[1,64]{1,0:T(1,128)} %bitcast.2, s32[1,64]{1,0:T(1,128)} %bitcast.3, s32[1]{0:T(128)S(6)} %copy.13.count), custom_call_target="tpu_custom_call" | custom-call | tf_op jit(solution)/shard_map/pack/pallas_call | solution.py:78
  2.2 4.0 %collective-permute-start.2 = (bf16[8,1536]{1,0:T(8,128)(2,1)S(1)}, bf16[8,1536]{1,0:T(8,128)(2,1)S(1)}, u32[]{:S(2)}, u32[]{:S(2)}) collective-permute-start(bf16[8,1536]{1,0:T(8,128)(2,1)S(1)} %pack.1.packet_ref.refs_0_), channel_id=1, source_target_pairs={{0,3},{1,2},{2,1},{3,0},{4,7},{5,6},{6,5},{7,4},{8,11},{9,10},{10,... | collective-permute-start | bytes 73736 | tf_op jit(solution)/shard_map/ppermute | solution.py:438
  6.2 0.5 %collective-permute-start.1 = (bf16[8,1536]{1,0:T(8,128)(2,1)S(1)}, bf16[8,1536]{1,0:T(8,128)(2,1)S(1)}, u32[]{:S(2)}, u32[]{:S(2)}) collective-permute-start(bf16[8,1536]{1,0:T(8,128)(2,1)S(1)} %pack.1.packet_ref.refs_0_), channel_id=1, source_target_pairs={{0,2},{1,3},{2,0},{3,1},{4,6},{5,7},{6,4},{7,5},{8,10},{9,11},{10,... | collective-permute-start | bytes 73736 | tf_op jit(solution)/shard_map/ppermute | solution.py:438
  6.7 0.1 collective-permute-start
  6.8 0.0 copy-done.1
  6.8 0.0 copy-done
  6.8 4.2 %conv_norm.1 = (bf16[512,1536]{1,0:T(8,128)(2,1)S(1)}, bf16[512,1536]{1,0:T(8,128)(2,1)S(1)}, bf16[1536,1536]{1,0:T(8,128)(2,1)S(1)}, bf16[256,128]{1,0:T(8,128)(2,1)S(1)}) custom-call(bf16[8,1536]{1,0:T(8,128)(2,1)S(1)} %pack.1.packet_ref.refs_0_, bf16[512,1536]{1,0:T(8,128)(2,1)} %feat_hbm.3, f32[5,1536]{1,0:T(8,128)S(1)} %copy-done, ...), custom_call_target="tpu_custom_call" | custom-call | flops 23592960 | bytes 12582912 | tf_op jit(solution)/shard_map/conv_norm/pallas_call | solution.py:222
  11.1 0.0 collective-permute-done.2.refs_3_
  11.1 0.0 collective-permute-done.1.refs_2_
  11.1 0.0 collective-permute-done.refs_1_
  11.1 6.6 %named_rows.1 = (bf16[64,768]{1,0:T(8,128)(2,1)S(1)}, bf16[64,768]{1,0:T(8,128)(2,1)S(1)}, bf16[64,768]{1,0:T(8,128)(2,1)S(1)}, bf16[64,768]{1,0:T(8,128)(2,1)S(1)}, bf16[512,1536]{1,0:T(8,128)(2,1)S(1)}) custom-call(bf16[8,1536]{1,0:T(8,128)(2,1)S(1)} %pack.1.packet_ref.refs_0_, ...), custom_call_target="tpu_custom_call", output_to_operand_aliasing={{4}: (5, {})} | custom-call | flops 3221225472 | bytes 8388608 | tf_op jit(solution)/shard_map/named_rows/pallas_call | solution.py:344
  17.7 2.0 %collective-permute-start.3 = (bf16[64,768]{1,0:T(8,128)(2,1)S(1)}, bf16[64,768]{1,0:T(8,128)(2,1)S(1)}, u32[]{:S(2)}, u32[]{:S(2)}) collective-permute-start(bf16[64,768]{1,0:T(8,128)(2,1)S(1)} %get-tuple-element.16), channel_id=1, source_target_pairs={{0,1},{1,0},{2,3},{3,2},{4,5},{5,4},{6,7},{7,6},{8,9},{9,8},{10,11... | collective-permute-start | bytes 294920 | tf_op jit(solution)/shard_map/ppermute | solution.py:438
  19.6 1.5 %collective-permute-start.4 = (bf16[64,768]{1,0:T(8,128)(2,1)S(1)}, bf16[64,768]{1,0:T(8,128)(2,1)S(1)}, u32[]{:S(2)}, u32[]{:S(2)}) collective-permute-start(bf16[64,768]{1,0:T(8,128)(2,1)S(1)} %get-tuple-element.17), channel_id=1, source_target_pairs={{0,2},{1,3},{2,0},{3,1},{4,6},{5,7},{6,4},{7,5},{8,10},{9,11},{10,... | collective-permute-start | bytes 294920 | tf_op jit(solution)/shard_map/ppermute | solution.py:438
  21.2 0.1 collective-permute-start.5
  21.2 5.1 %encode.1 = bf16[512,1536]{1,0:T(8,128)(2,1)} custom-call(bf16[512,1536]{1,0:T(8,128)(2,1)S(1)} %get-tuple-element.14.normed_ref, bf16[512,1536]{1,0:T(8,128)(2,1)S(1)} %get-tuple-element.11.refs_4_.feat_ref, bf16[1536,1536]{1,0:T(8,128)(2,1)S(1)} %get-tuple-element.13.refs_8_.w_ref), custom_call_target="tpu_custom_call" | custom-call | flops 2415919104 | bytes 8388608 | tf_op jit(solution)/shard_map/encode/pallas_call | solution.py:391
  26.3 0.0 collective-permute-done.3.refs_1_
  26.3 0.0 collective-permute-done.4.refs_2_
  26.4 0.3 %collective-permute-done.5.refs_3_ = bf16[64,768]{1,0:T(8,128)(2,1)S(1)} collective-permute-done((bf16[64,768]{1,0:T(8,128)(2,1)S(1)}, bf16[64,768]{1,0:T(8,128)(2,1)S(1)}, u32[]{:S(2)}, u32[]{:S(2)}) %collective-permute-start.5) | collective-permute-done | bytes 98336 | tf_op jit(solution)/shard_map/ppermute | solution.py:438
  26.7 1.0 %junction.1 = bf16[64,768]{1,0:T(8,128)(2,1)} custom-call(bf16[64,768]{1,0:T(8,128)(2,1)S(1)} %get-tuple-element.15.refs_0_, bf16[64,768]{1,0:T(8,128)(2,1)S(1)} %collective-permute-done.3.refs_1_, bf16[64,768]{1,0:T(8,128)(2,1)S(1)} %collective-permute-done.4.refs_2_, bf16[64,768]{1,0:T(8,128)(2,1)S(1)} %collective-permute-done.5.refs_3_, ...), custom_call_target="tpu_custom_call" | custom-call | tf_op jit(solution)/shard_map/junction/pallas_call | solution.py:427
  (1 shorter events, 0.0 us)
Async XLA Ops:
  0.6 6.2 %copy-start.1 = (f32[1536]{0:T(1024)S(1)}, f32[1536]{0:T(1024)}, u32[]{:S(2)}) copy-start(f32[1536]{0:T(1024)} %param.11) | copy-start | bytes 18436
  0.6 6.2 %copy-start = (f32[5,1536]{1,0:T(8,128)S(1)}, f32[5,1536]{1,0:T(8,128)}, u32[]{:S(2)}) copy-start(f32[5,1536]{1,0:T(8,128)} %refs_6_.1) | copy-start | bytes 92164
  2.2 8.9 %collective-permute-start.2 = (bf16[8,1536]{1,0:T(8,128)(2,1)S(1)}, bf16[8,1536]{1,0:T(8,128)(2,1)S(1)}, u32[]{:S(2)}, u32[]{:S(2)}) collective-permute-start(bf16[8,1536]{1,0:T(8,128)(2,1)S(1)} %pack.1.packet_ref.refs_0_), channel_id=1, source_target_pairs={{0,3},{1,2},{2,1},{3,0},{4,7},{5,6},{6,5},{7,4},{8,11},{9,10},{10,... | collective-permute-start | bytes 73736 | tf_op jit(solution)/shard_map/ppermute | solution.py:438
  6.2 4.9 %collective-permute-start.1 = (bf16[8,1536]{1,0:T(8,128)(2,1)S(1)}, bf16[8,1536]{1,0:T(8,128)(2,1)S(1)}, u32[]{:S(2)}, u32[]{:S(2)}) collective-permute-start(bf16[8,1536]{1,0:T(8,128)(2,1)S(1)} %pack.1.packet_ref.refs_0_), channel_id=1, source_target_pairs={{0,2},{1,3},{2,0},{3,1},{4,6},{5,7},{6,4},{7,5},{8,10},{9,11},{10,... | collective-permute-start | bytes 73736 | tf_op jit(solution)/shard_map/ppermute | solution.py:438
  6.7 4.4 %collective-permute-start = (bf16[8,1536]{1,0:T(8,128)(2,1)S(1)}, bf16[8,1536]{1,0:T(8,128)(2,1)S(1)}, u32[]{:S(2)}, u32[]{:S(2)}) collective-permute-start(bf16[8,1536]{1,0:T(8,128)(2,1)S(1)} %pack.1.packet_ref.refs_0_), channel_id=1, source_target_pairs={{0,1},{1,0},{2,3},{3,2},{4,5},{5,4},{6,7},{7,6},{8,9},{9,8},{10,11... | collective-permute-start | bytes 73736 | tf_op jit(solution)/shard_map/ppermute | solution.py:438
  17.7 8.6 %collective-permute-start.3 = (bf16[64,768]{1,0:T(8,128)(2,1)S(1)}, bf16[64,768]{1,0:T(8,128)(2,1)S(1)}, u32[]{:S(2)}, u32[]{:S(2)}) collective-permute-start(bf16[64,768]{1,0:T(8,128)(2,1)S(1)} %get-tuple-element.16), channel_id=1, source_target_pairs={{0,1},{1,0},{2,3},{3,2},{4,5},{5,4},{6,7},{7,6},{8,9},{9,8},{10,11... | collective-permute-start | bytes 294920 | tf_op jit(solution)/shard_map/ppermute | solution.py:438
  19.6 6.7 %collective-permute-start.4 = (bf16[64,768]{1,0:T(8,128)(2,1)S(1)}, bf16[64,768]{1,0:T(8,128)(2,1)S(1)}, u32[]{:S(2)}, u32[]{:S(2)}) collective-permute-start(bf16[64,768]{1,0:T(8,128)(2,1)S(1)} %get-tuple-element.17), channel_id=1, source_target_pairs={{0,2},{1,3},{2,0},{3,1},{4,6},{5,7},{6,4},{7,5},{8,10},{9,11},{10,... | collective-permute-start | bytes 294920 | tf_op jit(solution)/shard_map/ppermute | solution.py:438
  21.2 5.5 %collective-permute-start.5 = (bf16[64,768]{1,0:T(8,128)(2,1)S(1)}, bf16[64,768]{1,0:T(8,128)(2,1)S(1)}, u32[]{:S(2)}, u32[]{:S(2)}) collective-permute-start(bf16[64,768]{1,0:T(8,128)(2,1)S(1)} %get-tuple-element.18), channel_id=1, source_target_pairs={{0,3},{1,2},{2,1},{3,0},{4,7},{5,6},{6,5},{7,4},{8,11},{9,10},{10,... | collective-permute-start | bytes 294920 | tf_op jit(solution)/shard_map/ppermute | solution.py:438

commit v2 on v1

v2 whole, which is shorter than its diff:
```python
import functools

import jax
import jax.numpy as jnp
from jax import lax
from jax.experimental import pallas as pl
from jax.experimental.pallas import tpu as pltpu
from jax.sharding import PartitionSpec as P


F32 = jnp.float32
BF16 = jnp.bfloat16
LANES = 128
HALO = 2
MIB = 1 << 20


def vmem(shape, dtype):
    return pltpu.VMEM(shape, dtype)


def whole():
    return pl.BlockSpec(memory_space=pltpu.VMEM)


def far(array):
    return pltpu.with_memory_space_constraint(array, pltpu.MemorySpace.HBM)


def in_hbm():
    return pl.BlockSpec(memory_space=pltpu.MemorySpace.HBM)


def params(mib):
    return pltpu.CompilerParams(vmem_limit_bytes=mib * MIB)


def gelu(v):
    m = jnp.abs(v)
    d = m * F32(0.3275911 * 0.7071067811865476) + F32(1.0)
    u = pl.reciprocal(d, approx=False)
    p = u * F32(0.5 * 1.061405429) + F32(0.5 * -1.453152027)
    p = p * u + F32(0.5 * 1.421413741)
    p = p * u + F32(0.5 * -0.284496736)
    p = p * u + F32(0.5 * 0.254829592)
    e = jnp.exp2(v * v * F32(-0.5 * 1.4426950408889634))
    return jnp.maximum(v, F32(0.0)) - (m * u) * (p * e)


PIECES = 3
LINE = HALO * PIECES


def pack_kernel(owners, feat_hbm, donor_hbm, accept_hbm, count, *refs):
    outs = refs[:owners]
    ends, donor, accept, sides, sem = refs[owners:]
    rows, channels = feat_hbm.shape
    piece = channels // PIECES
    loads = [
        pltpu.make_async_copy(feat_hbm.at[pl.ds(0, 8)], ends.at[0], sem.at[0]),
        pltpu.make_async_copy(feat_hbm.at[pl.ds(rows - 8, 8)], ends.at[1], sem.at[1]),
        pltpu.make_async_copy(donor_hbm, donor, sem.at[2]),
        pltpu.make_async_copy(accept_hbm, accept, sem.at[3]),
    ]
    for load in loads:
        load.start()
    for load in loads:
        load.wait()
    wanted = jnp.concatenate([donor[...], accept[...]], axis=1)
    width = wanted.shape[1]
    live = jnp.full((1, width), count[0], jnp.int32)
    line = jnp.concatenate([wanted >> 8, wanted & 255, live], axis=1).astype(F32)
    line = jnp.concatenate([line, jnp.zeros((1, piece - 3 * width), F32)], axis=1)
    for side, top in ((0, 0), (1, 8 - HALO)):
        end = ends[side].astype(F32)
        for h in range(HALO):
            for c in range(PIECES):
                place = h * PIECES + c
                sides[side, place : place + 1, :] = end[top + h : top + h + 1, c * piece : (c + 1) * piece]
        sides[side, LINE : LINE + 1, :] = line
        sides[side, LINE + 1 : 8, :] = jnp.zeros((8 - LINE - 1, piece), F32)
    first = sides[0]
    last = sides[1]
    me = lax.axis_index("seq")
    for k in range(owners):
        outs[k][...] = jnp.where((me ^ k) == me + 1, last, first).astype(BF16)


def pack(features, donor, accept, count, owners):
    rows, channels = features.shape
    slots = donor.shape[0]
    piece = channels // PIECES
    return pl.pallas_call(
        functools.partial(pack_kernel, owners),
        in_specs=[in_hbm()] * 3 + [pl.BlockSpec(memory_space=pltpu.SMEM)],
        out_specs=[whole()] * owners,
        out_shape=[vmem((8, piece), BF16)] * owners,
        scratch_shapes=[
            pltpu.VMEM((2, 8, channels), BF16),
            pltpu.VMEM((1, slots), jnp.int32),
            pltpu.VMEM((1, slots), jnp.int32),
            pltpu.VMEM((2, 8, piece), F32),
            pltpu.SemaphoreType.DMA((4,)),
        ],
        compiler_params=params(4),
        cost_estimate=pl.CostEstimate(flops=20000 * rows * channels, bytes_accessed=1 << 20, transcendentals=0),
        name="pack",
    )(far(features), far(donor.reshape(1, slots)), far(accept.reshape(1, slots)), count)


def unpack_line(packet_ref, width):
    line = packet_ref[...].astype(F32)[LINE : LINE + 1, 0 : 3 * width]
    wanted = line[:, 0:width] * F32(256.0) + line[:, width : 2 * width]
    lane = lax.broadcasted_iota(jnp.int32, (1, width), 1)
    slot = jnp.where(lane >= width // 2, lane - width // 2, lane).astype(F32)
    return wanted, slot < line[:, 2 * width :]


def strict_upper(size):
    a = lax.broadcasted_iota(jnp.int32, (size, size), 0)
    b = lax.broadcasted_iota(jnp.int32, (size, size), 1)
    return (a < b).astype(F32).astype(BF16)


def chosen(mine, capacity):
    ranks = jnp.dot(mine.astype(BF16), strict_upper(mine.shape[1]), preferred_element_type=F32)
    keyed = jnp.where(mine > F32(0.5), ranks, F32(-1.0))
    level = lax.broadcasted_iota(jnp.int32, (capacity, mine.shape[1]), 0).astype(F32)
    return lambda k: keyed[k : k + 1, :] == level


def conv_rows(load, taps_ref, gain_ref, columns, eps_scale):
    tap_count = taps_ref.shape[0]
    held = []
    total = None
    for j in range(columns):
        lanes = slice(j * LANES, (j + 1) * LANES)
        acc = None
        for k in range(tap_count):
            term = taps_ref[k : k + 1, lanes] * load(j, k)
            acc = term if acc is None else acc + term
        held.append(acc)
        total = acc * acc if total is None else total + acc * acc
    mean = jnp.sum(total, axis=-1, keepdims=True) * F32(eps_scale)
    scale = lax.rsqrt(mean + F32(1e-06))
    return [
        (held[j] * scale * gain_ref[0:1, j * LANES : (j + 1) * LANES]).astype(BF16)
        for j in range(columns)
    ]


def conv_kernel(
    owners,
    capacity,
    width,
    packet_ref,
    feat_ref,
    taps_ref,
    gain_ref,
    w_hbm,
    wd_ref,
    wa_ref,
    normed_ref,
    w_ref,
    spread_ref,
    wide,
    weight_sem,
):
    del wd_ref, wa_ref
    rows, channels = feat_ref.shape
    columns = channels // LANES
    parts = 4
    step = rows // parts
    weights = [pltpu.make_async_copy(w_hbm, w_ref, weight_sem.at[0])]
    for load in weights:
        load.start()

    me = lax.axis_index("seq")
    wanted, live = unpack_line(packet_ref, width)
    group = lax.broadcasted_iota(jnp.int32, (max(8, owners), width), 0)
    low = ((group ^ me) * rows).astype(F32)
    here = (wanted >= low) & (wanted < low + F32(rows)) & live & (group < owners)
    pick = chosen(jnp.where(here, F32(1.0), F32(0.0)), capacity)
    for k in range(owners):
        spread_ref[k * capacity : (k + 1) * capacity, :] = jnp.where(
            pick(k), F32(1.0), F32(0.0)
        ).astype(BF16)

    edge = jnp.zeros((8, LANES), F32)
    for j in range(columns):
        wide[j, 0:8, :] = edge
        wide[j, rows + 8 : rows + 16, :] = edge

    tile = 32

    def widen(c):
        for j in range(columns):
            lanes = slice(j * LANES, (j + 1) * LANES)
            wide[j, 8 + c * step : 8 + (c + 1) * step, :] = feat_ref[
                c * step : (c + 1) * step, lanes
            ].astype(F32)

    def convolve(first, count):
        def body(i, carry):
            base = pl.multiple_of(first + i * tile, tile)

            def load(j, k):
                return wide.at[j, pl.ds(base, tile + 16), :][8 - HALO + k : 8 - HALO + k + tile, :]

            out = conv_rows(load, taps_ref, gain_ref, columns, 1.0 / channels)
            for j in range(columns):
                normed_ref[pl.ds(base, tile), j * LANES : (j + 1) * LANES] = out[j]
            return carry

        lax.fori_loop(0, count, body, 0)

    widen(0)
    done = 0
    for c in range(1, parts):
        widen(c)
        ready = c * step // tile * tile
        convolve(done, (ready - done) // tile)
        done = ready
    convolve(done, (rows - done) // tile)
    for load in weights:
        load.wait()


def conv_norm(packet, features, taps, gain, w, wd, wa, owners, capacity, width):
    rows, channels = features.shape
    return pl.pallas_call(
        functools.partial(conv_kernel, owners, capacity, width),
        in_specs=[whole(), whole(), whole(), whole(), in_hbm(), whole(), whole()],
        out_specs=[whole()] * 3,
        out_shape=[
            vmem((rows, channels), BF16),
            vmem(w.shape, BF16),
            vmem((owners * capacity, width), BF16),
        ],
        scratch_shapes=[
            pltpu.VMEM((channels // LANES, rows + 16, LANES), F32),
            pltpu.SemaphoreType.DMA((1,)),
        ],
        compiler_params=params(6),
        cost_estimate=pl.CostEstimate(flops=20000 * rows * channels, bytes_accessed=12 << 20, transcendentals=rows),
        name="conv_norm",
    )(packet, features, taps, gain.reshape(1, channels), far(w), wd, wa)


def named_kernel(owners, capacity, width, *refs):
    packets = refs[:owners]
    feat_ref, normed_ref, taps_ref, gain_ref, w_ref, wd_ref, wa_ref = refs[owners : owners + 7]
    outs = refs[owners + 7 : 2 * owners + 7]
    patched_ref = refs[2 * owners + 7]
    near, lhs, res, enc, proj = refs[2 * owners + 8 :]
    del normed_ref
    rows, channels = feat_ref.shape
    columns = channels // LANES
    heads = wd_ref.shape[1]
    block = lhs.shape[0]
    me = lax.axis_index("seq")

    groups = max(8, owners)
    group = lax.broadcasted_iota(jnp.int32, (groups, width), 0)
    lane = lax.broadcasted_iota(jnp.int32, (1, width), 1)
    local = jnp.zeros((groups, width), F32)
    mine = jnp.zeros((groups, width), F32)
    start = (me * rows).astype(F32)
    for k in range(owners):
        at, live = unpack_line(packets[k], width)
        at = at - start
        here = (at >= F32(0.0)) & (at < F32(rows)) & live
        mine = jnp.where(group == k, jnp.where(here, F32(1.0), F32(0.0)), mine)
        local = jnp.where(group == k, at, local)
    ranks = jnp.dot(mine.astype(BF16), strict_upper(width), preferred_element_type=F32)
    sizes = jnp.sum(mine, axis=1, keepdims=True)
    total = jnp.sum(mine)
    blocks = (total.astype(jnp.int32) + (block - 1)) // block
    mark = F32(1 << 16)
    code = local + F32(1.0) + jnp.where(lane >= width // 2, mark, F32(0.0))
    offsets = []
    spots = []
    running = jnp.zeros((1, 1), F32)
    for k in range(owners):
        offsets.append(running)
        spots.append(jnp.where(mine[k : k + 1] > F32(0.5), ranks[k : k + 1] + running, F32(-1.0)))
        running = running + sizes[k : k + 1]

    piece = packets[0].shape[1]
    above = jnp.zeros((8, piece), F32)
    below = jnp.zeros((8, piece), F32)
    for k in range(1, owners):
        other = packets[k][...].astype(F32)
        above = jnp.where((me ^ k) == me - 1, other, above)
        below = jnp.where((me ^ k) == me + 1, other, below)
    span = 16
    foot_at = 16 + span
    after_at = foot_at + span + 8
    for j in range(columns):
        lanes = slice(j * LANES, (j + 1) * LANES)
        near[j, 8:foot_at, :] = feat_ref[0 : span + 8, lanes].astype(F32)
        near[j, foot_at:after_at, :] = feat_ref[rows - span - 8 : rows, lanes].astype(F32)
        part = j * LANES // piece
        inner = slice(j * LANES - part * piece, (j + 1) * LANES - part * piece)
        for h in range(HALO):
            row = h * PIECES + part
            near[j, 8 - HALO + h : 9 - HALO + h, :] = above[row : row + 1, inner]
            near[j, after_at + h : after_at + h + 1, :] = below[row : row + 1, inner]
    for origin, place in ((8, 0), (foot_at + 8, rows - span)):

        def load(j, k, origin=origin):
            begin = origin - HALO + k
            return near[j, begin : begin + span, :]

        out = conv_rows(load, taps_ref, gain_ref, columns, 1.0 / channels)
        for j in range(columns):
            patched_ref[place : place + span, j * LANES : (j + 1) * LANES] = out[j]

    for k in range(owners):
        outs[k][...] = jnp.zeros((capacity, heads), BF16)

    spread = lax.broadcasted_iota(jnp.int32, (block, rows), 1).astype(F32)
    level = lax.broadcasted_iota(jnp.int32, (block, width), 0).astype(F32)
    slot = lax.broadcasted_iota(jnp.int32, (capacity, block), 0).astype(F32)
    column = lax.broadcasted_iota(jnp.int32, (capacity, block), 1).astype(F32)
    wide = 256

    def body(c, carry):
        base = (c * block).astype(F32)
        found = jnp.zeros((block, width), F32)
        for k in range(owners):
            found = jnp.where(spots[k] - base == level, code[k : k + 1, :], found)
        found = jnp.sum(found, axis=1, keepdims=True)
        accepts = found >= mark
        index = found - jnp.where(accepts, mark, F32(0.0)) - F32(1.0)
        grab = jnp.where(spread == index, F32(1.0), F32(0.0)).astype(BF16)
        for j in range(channels // wide):
            lanes = slice(j * wide, (j + 1) * wide)
            lhs[:, lanes] = jnp.dot(grab, patched_ref[:, lanes], preferred_element_type=F32).astype(BF16)
            res[:, lanes] = jnp.dot(grab, feat_ref[:, lanes], preferred_element_type=F32).astype(BF16)
        for j in range(channels // wide):
            lanes = slice(j * wide, (j + 1) * wide)
            mixed = jnp.dot(lhs[...], w_ref[:, lanes], preferred_element_type=F32)
            enc[:, lanes] = (res[:, lanes].astype(F32) + gelu(mixed)).astype(BF16)
        for j in range(heads // wide):
            lanes = slice(j * wide, (j + 1) * wide)
            left = jnp.dot(enc[...], wd_ref[:, lanes], preferred_element_type=F32)
            right = jnp.dot(enc[...], wa_ref[:, lanes], preferred_element_type=F32)
            proj[:, lanes] = jnp.where(accepts, right, left).astype(BF16)
        for k in range(owners):
            put = (column + base == offsets[k] + slot) & (slot < sizes[k : k + 1])
            put = jnp.where(put, F32(1.0), F32(0.0)).astype(BF16)
            placed = jnp.dot(put, proj[...], preferred_element_type=F32)
            outs[k][...] = (outs[k][...].astype(F32) + placed).astype(BF16)
        return carry

    lax.fori_loop(0, blocks, body, 0)


def named(packets, feat, normed, taps, gain, w, wd, wa, width, capacity):
    owners = len(packets)
    rows, channels = feat.shape
    heads = wd.shape[1]
    block = 128
    out = pl.pallas_call(
        functools.partial(named_kernel, owners, capacity, width),
        in_specs=[whole()] * (owners + 7),
        out_specs=[whole()] * (owners + 1),
        out_shape=[vmem((capacity, heads), BF16)] * owners + [vmem((rows, channels), BF16)],
        input_output_aliases={owners + 1: owners},
        scratch_shapes=[
            pltpu.VMEM((channels // LANES, 72, LANES), F32),
            pltpu.VMEM((block, channels), BF16),
            pltpu.VMEM((block, channels), BF16),
            pltpu.VMEM((block, channels), BF16),
            pltpu.VMEM((block, heads), BF16),
        ],
        compiler_params=params(16),
        cost_estimate=pl.CostEstimate(
            flops=8 * block * channels * (channels + rows), bytes_accessed=8 << 20, transcendentals=2 * block * channels
        ),
        name="named_rows",
    )(*packets, feat, normed, taps, gain.reshape(1, channels), w, wd, wa)
    return out[:owners], out[owners]


def encode_kernel(normed_ref, feat_ref, w_ref, out_hbm, stage, sem):
    rows, channels = feat_ref.shape
    wide = 256
    tall = 512
    copies = []
    tall = rows // 2
    for i in range(2):
        part = slice(i * tall, (i + 1) * tall)
        for j in range(channels // wide):
            lanes = slice(j * wide, (j + 1) * wide)
            mixed = jnp.dot(normed_ref[part, :], w_ref[:, lanes], preferred_element_type=F32)
            stage[part, lanes] = (feat_ref[part, lanes].astype(F32) + gelu(mixed)).astype(BF16)
            if j % 2 == 1:
                at = pl.ds((j - 1) * wide, 2 * wide)
                copy = pltpu.make_async_copy(
                    stage.at[pl.ds(i * tall, tall), at], out_hbm.at[pl.ds(i * tall, tall), at], sem.at[i * 3 + j // 2]
                )
                copy.start()
                copies.append(copy)
    for copy in copies:
        copy.wait()


def encode(normed, feat, w):
    rows, channels = feat.shape
    return pl.pallas_call(
        encode_kernel,
        in_specs=[whole()] * 3,
        out_specs=pl.BlockSpec(memory_space=pltpu.MemorySpace.HBM),
        out_shape=jax.ShapeDtypeStruct((rows, channels), BF16),
        scratch_shapes=[pltpu.VMEM((rows, channels), BF16), pltpu.SemaphoreType.DMA((channels // 256,))],
        compiler_params=params(6),
        cost_estimate=pl.CostEstimate(
            flops=2 * rows * channels * channels, bytes_accessed=8 << 20, transcendentals=2 * rows * channels
        ),
        name="encode",
    )(normed, feat, w)


def junction_kernel(owners, *refs):
    blocks = refs[:owners]
    spread_ref, out_ref = refs[owners:]
    slots = out_ref.shape[0]
    capacity = blocks[0].shape[0]
    picked = None
    for k in range(owners):
        part = lax.dot_general(
            spread_ref[k * capacity : (k + 1) * capacity, :],
            blocks[k][...],
            (((0,), (0,)), ((), ())),
            preferred_element_type=F32,
        )
        picked = part if picked is None else picked + part
    left, right = picked[:slots], picked[slots:]
    silu = left / (F32(1.0) + jnp.exp(-left))
    out_ref[...] = (silu * right).astype(BF16)


def junction(blocks, spread):
    slots = spread.shape[1] // 2
    heads = blocks[0].shape[1]
    return pl.pallas_call(
        functools.partial(junction_kernel, len(blocks)),
        in_specs=[whole()] * (len(blocks) + 1),
        out_specs=whole(),
        out_shape=jax.ShapeDtypeStruct((slots, heads), BF16),
        compiler_params=params(6),
        name="junction",
    )(*blocks, spread)


def swap_all(arrays):
    owners = len(arrays)
    got = [arrays[0]]
    for k in range(1, owners):
        got.append(lax.ppermute(arrays[k], "seq", [(i, i ^ k) for i in range(owners)]))
    return got


def on_device(
    features,
    conv_taps,
    norm_gain,
    point_weight,
    donor_weight,
    accept_weight,
    donor_pos,
    accept_pos,
    pair_counts,
):
    slots = donor_pos.shape[0]
    owners = lax.axis_size("seq")
    capacity = 2 * ((2 * slots + owners - 1) // owners)
    own = pack(features, donor_pos, accept_pos, pair_counts, owners)
    packets = swap_all(own)
    width = 2 * slots
    normed, w, spread = conv_norm(
        own[0], features, conv_taps, norm_gain, point_weight, donor_weight, accept_weight, owners, capacity, width
    )
    sends, patched = named(
        packets, features, normed, conv_taps, norm_gain, w, donor_weight, accept_weight, width, capacity
    )
    blocks = swap_all(sends)
    encoded = encode(patched, features, w)
    return encoded, junction(blocks, spread)


def solution(mesh):
    placed = (
        P(("dp", "seq"), None),
        P(),
        P(),
        P(),
        P(),
        P(),
        P(("dp", "seq")),
        P(("dp", "seq")),
        P(("dp", "seq")),
    )

    return jax.shard_map(
        on_device,
        mesh=mesh,
        in_specs=placed,
        out_specs=(P(("dp", "seq"), None), P(("dp", "seq"), None)),
        check_vma=False,
    )
```

time: 28 us -> 24.2 us (0.86)
  Pallas kernels: 17.8 us -> 13.2 us
  waiting for transfers between devices: 0.34 us -> 1.3 us
    pallas_call x1, Pallas kernels: 6.59 us -> 2.85 us  [named(): pl.pallas_call(functools.partial(named_kernel, owners, capacity, width),...]
    pallas_call x1, Pallas kernels: 4.21 us -> 3.16 us  [conv_norm(): pl.pallas_call(functools.partial(conv_kernel, owners, capacity, width), i...]
    ppermute x6, waiting for transfers between devices: 0.34 us -> 1.3 us  [swap_all(): lax.ppermute(arrays[k], 'seq', [(i, i ^ k) for i in range(owners)])]
where the time goes in v2:
time: 24.2 us; the launch traced here: 24.1 us
  Pallas kernels  13.2 us (55%)
  starting transfers between devices  8.13 us (34%)
  between operations  1.43 us (6%)
  waiting for transfers between devices  1.3 us (5%)
    ppermute x6, starting transfers between devices, swap_all(): lax.ppermute(arrays[k], 'seq', [(i, i ^ k) for i in range(owners)])  8.13 us
    pallas_call x1, Pallas kernels, encode(): pl.pallas_call(encode_kernel, in_specs=[whole()] * 3, out_specs=pl.BlockS...  5.13 us
    pallas_call x1, Pallas kernels, conv_norm(): pl.pallas_call(functools.partial(conv_kernel, owners, capacity, width), i...  3.16 us
    pallas_call x1, Pallas kernels, named(): pl.pallas_call(functools.partial(named_kernel, owners, capacity, width),...  2.85 us
    ppermute x6, waiting for transfers between devices, swap_all(): lax.ppermute(arrays[k], 'seq', [(i, i ^ k) for i in range(owners)])  1.3 us
    pallas_call x1, Pallas kernels, junction(): pl.pallas_call(functools.partial(junction_kernel, len(blocks)), in_specs=...  1.05 us
    pallas_call x1, Pallas kernels, pack(): pl.pallas_call(functools.partial(pack_kernel, owners), in_specs=[in_hbm()...  1.03 us
  transfers between devices with their start and end apart: 6, of which 1 were waited for; matrix products, arithmetic and copies ran while one was open for 0% of the time, Pallas kernels for 34%

profile of v2, /device:TPU:0, one launch (start us, length us, event | category | flops | bytes accessed | tf_op | source)
XLA Modules:
  0.0 24.1 jit_solution(9391167043054193808)
XLA Ops:
  1.3 0.0 copy-start.4
  1.3 0.0 copy-start
  1.3 0.0 copy-start.1
  1.3 0.0 copy-start.2
  1.3 0.0 copy-start.3
  1.3 1.0 %pack.1 = (bf16[8,512]{1,0:T(8,128)(2,1)S(1)}, bf16[8,512]{1,0:T(8,128)(2,1)S(1)}, bf16[8,512]{1,0:T(8,128)(2,1)S(1)}, bf16[8,512]{1,0:T(8,128)(2,1)S(1)}) custom-call(bf16[512,1536]{1,0:T(8,128)(2,1)} %feat_ref.3, s32[1,64]{1,0:T(1,128)} %bitcast.2, s32[1,64]{1,0:T(1,128)} %bitcast.3, s32[1]{0:T(128)S(6)} %copy.13.count), custom_call_target="tpu_custom_call" | custom-call | flops 15728640000 | bytes 1048576 | tf_op jit(solution)/shard_map/pack/pallas_call | solution.py:93
  2.4 3.0 %collective-permute-start = (bf16[8,512]{1,0:T(8,128)(2,1)S(1)}, bf16[8,512]{1,0:T(8,128)(2,1)S(1)}, u32[]{:S(2)}, u32[]{:S(2)}) collective-permute-start(bf16[8,512]{1,0:T(8,128)(2,1)S(1)} %get-tuple-element.15), channel_id=1, source_target_pairs={{0,1},{1,0},{2,3},{3,2},{4,5},{5,4},{6,7},{7,6},{8,9},{9,8},{10,11... | collective-permute-start | bytes 24584 | tf_op jit(solution)/shard_map/ppermute | solution.py:462
  5.4 1.5 %collective-permute-start.1 = (bf16[8,512]{1,0:T(8,128)(2,1)S(1)}, bf16[8,512]{1,0:T(8,128)(2,1)S(1)}, u32[]{:S(2)}, u32[]{:S(2)}) collective-permute-start(bf16[8,512]{1,0:T(8,128)(2,1)S(1)} %get-tuple-element.16), channel_id=1, source_target_pairs={{0,2},{1,3},{2,0},{3,1},{4,6},{5,7},{6,4},{7,5},{8,10},{9,11},{10,... | collective-permute-start | bytes 24584 | tf_op jit(solution)/shard_map/ppermute | solution.py:462
  6.9 0.0 collective-permute-start.2
  6.9 0.0 copy-done.4
  7.0 0.0 copy-done
  7.0 0.0 copy-done.1
  7.0 0.0 copy-done.2
  7.0 0.0 copy-done.3
  7.0 3.2 %conv_norm.1 = (bf16[512,1536]{1,0:T(8,128)(2,1)S(1)}, bf16[1536,1536]{1,0:T(8,128)(2,1)S(1)}, bf16[256,128]{1,0:T(8,128)(2,1)S(1)}) custom-call(bf16[8,512]{1,0:T(8,128)(2,1)S(1)} %get-tuple-element.14.packet_ref.refs_0_, bf16[512,1536]{1,0:T(8,128)(2,1)S(1)} %copy-done, f32[5,1536]{1,0:T(8,128)S(1)} %copy-done.3, f32[1,1536]{1,0:T(1,128)S(1)} %reshape.16.gain_ref.refs_7_, ...), custom_call_target="tpu_custom_call" | custom-call | flops 15728640000 | bytes 12582912 | tf_op jit(solution)/shard_map/conv_norm/pallas_call | solution.py:231
  10.2 0.0 collective-permute-done.refs_1_
  10.2 0.0 collective-permute-done.1.refs_2_
  10.2 1.3 %collective-permute-done.2.refs_3_ = bf16[8,512]{1,0:T(8,128)(2,1)S(1)} collective-permute-done((bf16[8,512]{1,0:T(8,128)(2,1)S(1)}, bf16[8,512]{1,0:T(8,128)(2,1)S(1)}, u32[]{:S(2)}, u32[]{:S(2)}) %collective-permute-start.2) | collective-permute-done | bytes 8224 | tf_op jit(solution)/shard_map/ppermute | solution.py:462
  11.5 2.8 %named_rows.1 = (bf16[64,768]{1,0:T(8,128)(2,1)S(1)}, bf16[64,768]{1,0:T(8,128)(2,1)S(1)}, bf16[64,768]{1,0:T(8,128)(2,1)S(1)}, bf16[64,768]{1,0:T(8,128)(2,1)S(1)}, bf16[512,1536]{1,0:T(8,128)(2,1)S(1)}) custom-call(bf16[8,512]{1,0:T(8,128)(2,1)S(1)} %get-tuple-element.14.packet_ref.refs_0_, ...), custom_call_target="tpu_custom_call", output_to_operand_aliasing={{4}: (5, {})} | custom-call | flops 3221225472 | bytes 8388608 | tf_op jit(solution)/shard_map/named_rows/pallas_call | solution.py:365
  14.3 0.7 %collective-permute-start.3 = (bf16[64,768]{1,0:T(8,128)(2,1)S(1)}, bf16[64,768]{1,0:T(8,128)(2,1)S(1)}, u32[]{:S(2)}, u32[]{:S(2)}) collective-permute-start(bf16[64,768]{1,0:T(8,128)(2,1)S(1)} %get-tuple-element.22), channel_id=1, source_target_pairs={{0,1},{1,0},{2,3},{3,2},{4,5},{5,4},{6,7},{7,6},{8,9},{9,8},{10,11... | collective-permute-start | bytes 294920 | tf_op jit(solution)/shard_map/ppermute | solution.py:462
  15.1 1.5 %collective-permute-start.4 = (bf16[64,768]{1,0:T(8,128)(2,1)S(1)}, bf16[64,768]{1,0:T(8,128)(2,1)S(1)}, u32[]{:S(2)}, u32[]{:S(2)}) collective-permute-start(bf16[64,768]{1,0:T(8,128)(2,1)S(1)} %get-tuple-element.23), channel_id=1, source_target_pairs={{0,2},{1,3},{2,0},{3,1},{4,6},{5,7},{6,4},{7,5},{8,10},{9,11},{10,... | collective-permute-start | bytes 294920 | tf_op jit(solution)/shard_map/ppermute | solution.py:462
  16.6 1.3 %collective-permute-start.5 = (bf16[64,768]{1,0:T(8,128)(2,1)S(1)}, bf16[64,768]{1,0:T(8,128)(2,1)S(1)}, u32[]{:S(2)}, u32[]{:S(2)}) collective-permute-start(bf16[64,768]{1,0:T(8,128)(2,1)S(1)} %get-tuple-element.24), channel_id=1, source_target_pairs={{0,3},{1,2},{2,1},{3,0},{4,7},{5,6},{6,5},{7,4},{8,11},{9,10},{10,... | collective-permute-start | bytes 294920 | tf_op jit(solution)/shard_map/ppermute | solution.py:462
  17.9 5.1 %encode.1 = bf16[512,1536]{1,0:T(8,128)(2,1)} custom-call(bf16[512,1536]{1,0:T(8,128)(2,1)S(1)} %get-tuple-element.20.normed_ref, bf16[512,1536]{1,0:T(8,128)(2,1)S(1)} %copy-done, bf16[1536,1536]{1,0:T(8,128)(2,1)S(1)} %get-tuple-element.19.refs_8_.w_ref), custom_call_target="tpu_custom_call" | custom-call | flops 2415919104 | bytes 8388608 | tf_op jit(solution)/shard_map/encode/pallas_call | solution.py:412
  23.0 0.0 collective-permute-done.3.refs_1_
  23.0 0.0 collective-permute-done.4.refs_2_
  23.0 0.0 collective-permute-done.5.refs_3_
  23.0 1.1 %junction.1 = bf16[64,768]{1,0:T(8,128)(2,1)} custom-call(bf16[64,768]{1,0:T(8,128)(2,1)S(1)} %get-tuple-element.21.refs_0_, bf16[64,768]{1,0:T(8,128)(2,1)S(1)} %collective-permute-done.3.refs_1_, bf16[64,768]{1,0:T(8,128)(2,1)S(1)} %collective-permute-done.4.refs_2_, bf16[64,768]{1,0:T(8,128)(2,1)S(1)} %collective-permute-done.5.refs_3_, ...), custom_call_target="tpu_custom_call" | custom-call | tf_op jit(solution)/shard_map/junction/pallas_call | solution.py:448
  (1 shorter events, 0.0 us)
Async XLA Ops:
  1.3 5.7 %copy-start.4 = (f32[1536]{0:T(1024)S(1)}, f32[1536]{0:T(1024)}, u32[]{:S(2)}) copy-start(f32[1536]{0:T(1024)} %param.11) | copy-start | bytes 18436
  1.3 5.7 %copy-start = (bf16[512,1536]{1,0:T(8,128)(2,1)S(1)}, bf16[512,1536]{1,0:T(8,128)(2,1)}, u32[]{:S(2)}) copy-start(bf16[512,1536]{1,0:T(8,128)(2,1)} %feat_ref.3) | copy-start | bytes 4718596
  1.3 5.7 %copy-start.1 = (bf16[1536,768]{1,0:T(8,128)(2,1)S(1)}, bf16[1536,768]{1,0:T(8,128)(2,1)}, u32[]{:S(2)}) copy-start(bf16[1536,768]{1,0:T(8,128)(2,1)} %refs_9_.1) | copy-start | bytes 7077892
  1.3 5.7 %copy-start.2 = (bf16[1536,768]{1,0:T(8,128)(2,1)S(1)}, bf16[1536,768]{1,0:T(8,128)(2,1)}, u32[]{:S(2)}) copy-start(bf16[1536,768]{1,0:T(8,128)(2,1)} %refs_10_.1) | copy-start | bytes 7077892
  1.3 5.7 %copy-start.3 = (f32[5,1536]{1,0:T(8,128)S(1)}, f32[5,1536]{1,0:T(8,128)}, u32[]{:S(2)}) copy-start(f32[5,1536]{1,0:T(8,128)} %refs_6_.1) | copy-start | bytes 92164
  2.4 7.8 %collective-permute-start = (bf16[8,512]{1,0:T(8,128)(2,1)S(1)}, bf16[8,512]{1,0:T(8,128)(2,1)S(1)}, u32[]{:S(2)}, u32[]{:S(2)}) collective-permute-start(bf16[8,512]{1,0:T(8,128)(2,1)S(1)} %get-tuple-element.15), channel_id=1, source_target_pairs={{0,1},{1,0},{2,3},{3,2},{4,5},{5,4},{6,7},{7,6},{8,9},{9,8},{10,11... | collective-permute-start | bytes 24584 | tf_op jit(solution)/shard_map/ppermute | solution.py:462
  5.4 4.8 %collective-permute-start.1 = (bf16[8,512]{1,0:T(8,128)(2,1)S(1)}, bf16[8,512]{1,0:T(8,128)(2,1)S(1)}, u32[]{:S(2)}, u32[]{:S(2)}) collective-permute-start(bf16[8,512]{1,0:T(8,128)(2,1)S(1)} %get-tuple-element.16), channel_id=1, source_target_pairs={{0,2},{1,3},{2,0},{3,1},{4,6},{5,7},{6,4},{7,5},{8,10},{9,11},{10,... | collective-permute-start | bytes 24584 | tf_op jit(solution)/shard_map/ppermute | solution.py:462
  6.9 4.5 %collective-permute-start.2 = (bf16[8,512]{1,0:T(8,128)(2,1)S(1)}, bf16[8,512]{1,0:T(8,128)(2,1)S(1)}, u32[]{:S(2)}, u32[]{:S(2)}) collective-permute-start(bf16[8,512]{1,0:T(8,128)(2,1)S(1)} %get-tuple-element.17), channel_id=1, source_target_pairs={{0,3},{1,2},{2,1},{3,0},{4,7},{5,6},{6,5},{7,4},{8,11},{9,10},{10,... | collective-permute-start | bytes 24584 | tf_op jit(solution)/shard_map/ppermute | solution.py:462
  14.3 8.7 %collective-permute-start.3 = (bf16[64,768]{1,0:T(8,128)(2,1)S(1)}, bf16[64,768]{1,0:T(8,128)(2,1)S(1)}, u32[]{:S(2)}, u32[]{:S(2)}) collective-permute-start(bf16[64,768]{1,0:T(8,128)(2,1)S(1)} %get-tuple-element.22), channel_id=1, source_target_pairs={{0,1},{1,0},{2,3},{3,2},{4,5},{5,4},{6,7},{7,6},{8,9},{9,8},{10,11... | collective-permute-start | bytes 294920 | tf_op jit(solution)/shard_map/ppermute | solution.py:462
  15.1 8.0 %collective-permute-start.4 = (bf16[64,768]{1,0:T(8,128)(2,1)S(1)}, bf16[64,768]{1,0:T(8,128)(2,1)S(1)}, u32[]{:S(2)}, u32[]{:S(2)}) collective-permute-start(bf16[64,768]{1,0:T(8,128)(2,1)S(1)} %get-tuple-element.23), channel_id=1, source_target_pairs={{0,2},{1,3},{2,0},{3,1},{4,6},{5,7},{6,4},{7,5},{8,10},{9,11},{10,... | collective-permute-start | bytes 294920 | tf_op jit(solution)/shard_map/ppermute | solution.py:462
  16.6 6.5 %collective-permute-start.5 = (bf16[64,768]{1,0:T(8,128)(2,1)S(1)}, bf16[64,768]{1,0:T(8,128)(2,1)S(1)}, u32[]{:S(2)}, u32[]{:S(2)}) collective-permute-start(bf16[64,768]{1,0:T(8,128)(2,1)S(1)} %get-tuple-element.24), channel_id=1, source_target_pairs={{0,3},{1,2},{2,1},{3,0},{4,7},{5,6},{6,5},{7,4},{8,11},{9,10},{10,... | collective-permute-start | bytes 294920 | tf_op jit(solution)/shard_map/ppermute | solution.py:462

commit v3 on v2

--- a/solution.py
+++ b/solution.py
@@ -157,21 +157,21 @@
     feat_ref,
     taps_ref,
     gain_ref,
-    w_hbm,
+    w_ref,
     wd_ref,
+    wa_hbm,
+    normed_ref,
     wa_ref,
-    normed_ref,
-    w_ref,
     spread_ref,
     wide,
+    mixed,
+    squares,
     weight_sem,
 ):
-    del wd_ref, wa_ref
+    del w_ref, wd_ref
     rows, channels = feat_ref.shape
     columns = channels // LANES
-    parts = 4
-    step = rows // parts
-    weights = [pltpu.make_async_copy(w_hbm, w_ref, weight_sem.at[0])]
+    weights = [pltpu.make_async_copy(wa_hbm, wa_ref, weight_sem.at[0])]
     for load in weights:
         load.start()
 
@@ -192,36 +192,42 @@
         wide[j, rows + 8 : rows + 16, :] = edge
 
     tile = 32
-
-    def widen(c):
+    tap_count = taps_ref.shape[0]
+
+    for j in range(columns):
+        lanes = slice(j * LANES, (j + 1) * LANES)
+        wide[j, 8 : 8 + rows, :] = feat_ref[:, lanes].astype(F32)
+
+    def convolve(i, carry):
+        base = pl.multiple_of(i * tile, tile)
+        total = None
         for j in range(columns):
             lanes = slice(j * LANES, (j + 1) * LANES)
-            wide[j, 8 + c * step : 8 + (c + 1) * step, :] = feat_ref[
-                c * step : (c + 1) * step, lanes
-            ].astype(F32)
-
-    def convolve(first, count):
-        def body(i, carry):
-            base = pl.multiple_of(first + i * tile, tile)
-
-            def load(j, k):
-                return wide.at[j, pl.ds(base, tile + 16), :][8 - HALO + k : 8 - HALO + k + tile, :]
-
-            out = conv_rows(load, taps_ref, gain_ref, columns, 1.0 / channels)
-            for j in range(columns):
-                normed_ref[pl.ds(base, tile), j * LANES : (j + 1) * LANES] = out[j]
-            return carry
-
-        lax.fori_loop(0, count, body, 0)
-
-    widen(0)
-    done = 0
-    for c in range(1, parts):
-        widen(c)
-        ready = c * step // tile * tile
-        convolve(done, (ready - done) // tile)
-        done = ready
-    convolve(done, (rows - done) // tile)
+            acc = None
+            for k in range(tap_count):
+                begin = 8 - HALO + k
+                part = wide.at[j, pl.ds(base, tile + 16), :][begin : begin + tile, :]
+                term = taps_ref[k : k + 1, lanes] * part
+                acc = term if acc is None else acc + term
+            mixed[j, pl.ds(base, tile), :] = acc
+            total = acc * acc if total is None else total + acc * acc
+        squares[pl.ds(base, tile), :] = total
+        return carry
+
+    lax.fori_loop(0, rows // tile, convolve, 0, unroll=2)
+    mean = jnp.sum(squares[...], axis=-1, keepdims=True) * F32(1.0 / channels)
+    squares[...] = jnp.broadcast_to(lax.rsqrt(mean + F32(1e-06)), (rows, LANES))
+
+    def scale(i, carry):
+        base = pl.multiple_of(i * tile, tile)
+        by = squares[pl.ds(base, tile), :]
+        for j in range(columns):
+            lanes = slice(j * LANES, (j + 1) * LANES)
+            out = mixed[j, pl.ds(base, tile), :] * by * gain_ref[0:1, lanes]
+            normed_ref[pl.ds(base, tile), lanes] = out.astype(BF16)
+        return carry
+
+    lax.fori_loop(0, rows // tile, scale, 0)
     for load in weights:
         load.wait()
 
@@ -230,21 +236,23 @@
     rows, channels = features.shape
     return pl.pallas_call(
         functools.partial(conv_kernel, owners, capacity, width),
-        in_specs=[whole(), whole(), whole(), whole(), in_hbm(), whole(), whole()],
+        in_specs=[whole(), whole(), whole(), whole(), whole(), whole(), in_hbm()],
         out_specs=[whole()] * 3,
         out_shape=[
             vmem((rows, channels), BF16),
-            vmem(w.shape, BF16),
+            vmem(wa.shape, BF16),
             vmem((owners * capacity, width), BF16),
         ],
         scratch_shapes=[
             pltpu.VMEM((channels // LANES, rows + 16, LANES), F32),
+            pltpu.VMEM((channels // LANES, rows, LANES), F32),
+            pltpu.VMEM((rows, LANES), F32),
             pltpu.SemaphoreType.DMA((1,)),
         ],
-        compiler_params=params(6),
+        compiler_params=params(10),
         cost_estimate=pl.CostEstimate(flops=20000 * rows * channels, bytes_accessed=12 << 20, transcendentals=rows),
         name="conv_norm",
-    )(packet, features, taps, gain.reshape(1, channels), far(w), wd, wa)
+    )(packet, features, taps, gain.reshape(1, channels), w, wd, far(wa))
 
 
 def named_kernel(owners, capacity, width, *refs):
@@ -316,17 +324,14 @@
         for j in range(columns):
             patched_ref[place : place + span, j * LANES : (j + 1) * LANES] = out[j]
 
-    for k in range(owners):
-        outs[k][...] = jnp.zeros((capacity, heads), BF16)
-
     spread = lax.broadcasted_iota(jnp.int32, (block, rows), 1).astype(F32)
     level = lax.broadcasted_iota(jnp.int32, (block, width), 0).astype(F32)
     slot = lax.broadcasted_iota(jnp.int32, (capacity, block), 0).astype(F32)
     column = lax.broadcasted_iota(jnp.int32, (capacity, block), 1).astype(F32)
     wide = 256
 
-    def body(c, carry):
-        base = (c * block).astype(F32)
+    def encode_block(c, store):
+        base = F32(c * block) if isinstance(c, int) else (c * block).astype(F32)
         found = jnp.zeros((block, width), F32)
         for k in range(owners):
             found = jnp.where(spots[k] - base == level, code[k : k + 1, :], found)
@@ -351,10 +356,21 @@
             put = (column + base == offsets[k] + slot) & (slot < sizes[k : k + 1])
             put = jnp.where(put, F32(1.0), F32(0.0)).astype(BF16)
             placed = jnp.dot(put, proj[...], preferred_element_type=F32)
-            outs[k][...] = (outs[k][...].astype(F32) + placed).astype(BF16)
+            store(outs[k], placed)
+
+    def write(ref, value):
+        ref[...] = value.astype(BF16)
+
+    def add(ref, value):
+        ref[...] = (ref[...].astype(F32) + value).astype(BF16)
+
+    encode_block(0, write)
+
+    def body(c, carry):
+        encode_block(c, add)
         return carry
 
-    lax.fori_loop(0, blocks, body, 0)
+    lax.fori_loop(1, blocks, body, 0)
 
 
 def named(packets, feat, normed, taps, gain, w, wd, wa, width, capacity):
@@ -480,14 +496,14 @@
     own = pack(features, donor_pos, accept_pos, pair_counts, owners)
     packets = swap_all(own)
     width = 2 * slots
-    normed, w, spread = conv_norm(
+    normed, wa, spread = conv_norm(
         own[0], features, conv_taps, norm_gain, point_weight, donor_weight, accept_weight, owners, capacity, width
     )
     sends, patched = named(
-        packets, features, normed, conv_taps, norm_gain, w, donor_weight, accept_weight, width, capacity
+        packets, features, normed, conv_taps, norm_gain, point_weight, donor_weight, wa, width, capacity
     )
     blocks = swap_all(sends)
-    encoded = encode(patched, features, w)
+    encoded = encode(patched, features, point_weight)
     return encoded, junction(blocks, spread)
 
 

time: 24.2 us -> 24.2 us (level)
  Pallas kernels: 13.2 us -> 12 us
  waiting for transfers between devices: 1.3 us -> 2.45 us
    ppermute x6, waiting for transfers between devices: 1.3 us -> 2.45 us  [swap_all(): lax.ppermute(arrays[k], 'seq', [(i, i ^ k) for i in range(owners)])]
    pallas_call x1, Pallas kernels: 3.16 us -> 2.02 us  [conv_norm(): pl.pallas_call(functools.partial(conv_kernel, owners, capacity, width), i...]
  transfers between devices with their start and end apart: 6 -> 6, of which waited for: 1 -> 1; matrix products, arithmetic and copies ran while one was open for 0% -> 0% of each run, Pallas kernels for 34% -> 30%
where the time goes in v3:
time: 24.2 us; the launch traced here: 24 us
  Pallas kernels  12 us (50%)
  starting transfers between devices  8.13 us (34%)
  waiting for transfers between devices  2.45 us (10%)
  between operations  1.42 us (6%)
    ppermute x6, starting transfers between devices, swap_all(): lax.ppermute(arrays[k], 'seq', [(i, i ^ k) for i in range(owners)])  8.13 us
    pallas_call x1, Pallas kernels, encode(): pl.pallas_call(encode_kernel, in_specs=[whole()] * 3, out_specs=pl.BlockS...  5.13 us
    pallas_call x1, Pallas kernels, named(): pl.pallas_call(functools.partial(named_kernel, owners, capacity, width),...  2.77 us
    ppermute x6, waiting for transfers between devices, swap_all(): lax.ppermute(arrays[k], 'seq', [(i, i ^ k) for i in range(owners)])  2.45 us
    pallas_call x1, Pallas kernels, conv_norm(): pl.pallas_call(functools.partial(conv_kernel, owners, capacity, width), i...  2.02 us
    pallas_call x1, Pallas kernels, junction(): pl.pallas_call(functools.partial(junction_kernel, len(blocks)), in_specs=...  1.05 us
    pallas_call x1, Pallas kernels, pack(): pl.pallas_call(functools.partial(pack_kernel, owners), in_specs=[in_hbm()...  1.03 us
  transfers between devices with their start and end apart: 6, of which 1 were waited for; matrix products, arithmetic and copies ran while one was open for 0% of the time, Pallas kernels for 30%

profile of v3, /device:TPU:0, one launch (start us, length us, event | category | flops | bytes accessed | tf_op | source)
XLA Modules:
  0.0 24.0 jit_solution(9491471305713840239)
XLA Ops:
  1.3 0.0 copy-start.4
  1.3 0.0 copy-start
  1.3 0.0 copy-start.1
  1.3 0.0 copy-start.2
  1.3 0.0 copy-start.3
  1.3 1.0 %pack.1 = (bf16[8,512]{1,0:T(8,128)(2,1)S(1)}, bf16[8,512]{1,0:T(8,128)(2,1)S(1)}, bf16[8,512]{1,0:T(8,128)(2,1)S(1)}, bf16[8,512]{1,0:T(8,128)(2,1)S(1)}) custom-call(bf16[512,1536]{1,0:T(8,128)(2,1)} %feat_ref.3, s32[1,64]{1,0:T(1,128)} %bitcast.2, s32[1,64]{1,0:T(1,128)} %bitcast.3, s32[1]{0:T(128)S(6)} %copy.13.count), custom_call_target="tpu_custom_call" | custom-call | flops 15728640000 | bytes 1048576 | tf_op jit(solution)/shard_map/pack/pallas_call | solution.py:93
  2.4 3.0 %collective-permute-start = (bf16[8,512]{1,0:T(8,128)(2,1)S(1)}, bf16[8,512]{1,0:T(8,128)(2,1)S(1)}, u32[]{:S(2)}, u32[]{:S(2)}) collective-permute-start(bf16[8,512]{1,0:T(8,128)(2,1)S(1)} %get-tuple-element.15), channel_id=1, source_target_pairs={{0,1},{1,0},{2,3},{3,2},{4,5},{5,4},{6,7},{7,6},{8,9},{9,8},{10,11... | collective-permute-start | bytes 24584 | tf_op jit(solution)/shard_map/ppermute | solution.py:478
  5.4 1.5 %collective-permute-start.1 = (bf16[8,512]{1,0:T(8,128)(2,1)S(1)}, bf16[8,512]{1,0:T(8,128)(2,1)S(1)}, u32[]{:S(2)}, u32[]{:S(2)}) collective-permute-start(bf16[8,512]{1,0:T(8,128)(2,1)S(1)} %get-tuple-element.16), channel_id=1, source_target_pairs={{0,2},{1,3},{2,0},{3,1},{4,6},{5,7},{6,4},{7,5},{8,10},{9,11},{10,... | collective-permute-start | bytes 24584 | tf_op jit(solution)/shard_map/ppermute | solution.py:478
  6.9 0.0 collective-permute-start.2
  6.9 0.0 copy-done.4
  7.0 0.0 copy-done
  7.0 0.0 copy-done.1
  7.0 0.0 copy-done.2
  7.0 0.0 copy-done.3
  7.0 2.0 %conv_norm.1 = (bf16[512,1536]{1,0:T(8,128)(2,1)S(1)}, bf16[1536,768]{1,0:T(8,128)(2,1)S(1)}, bf16[256,128]{1,0:T(8,128)(2,1)S(1)}) custom-call(bf16[8,512]{1,0:T(8,128)(2,1)S(1)} %get-tuple-element.14.packet_ref.refs_0_, bf16[512,1536]{1,0:T(8,128)(2,1)S(1)} %copy-done.1, f32[5,1536]{1,0:T(8,128)S(1)} %copy-done.3, f32[1,1536]{1,0:T(1,128)S(1)} %reshape.16.gain_ref.refs_7_, ...), custom_call_target="tpu_custom_call" | custom-call | flops 15728640000 | bytes 12582912 | tf_op jit(solution)/shard_map/conv_norm/pallas_call | solution.py:237
  9.0 0.0 collective-permute-done.refs_1_
  9.0 0.0 collective-permute-done.1.refs_2_
  9.1 2.4 %collective-permute-done.2.refs_3_ = bf16[8,512]{1,0:T(8,128)(2,1)S(1)} collective-permute-done((bf16[8,512]{1,0:T(8,128)(2,1)S(1)}, bf16[8,512]{1,0:T(8,128)(2,1)S(1)}, u32[]{:S(2)}, u32[]{:S(2)}) %collective-permute-start.2) | collective-permute-done | bytes 8224 | tf_op jit(solution)/shard_map/ppermute | solution.py:478
  11.5 2.8 %named_rows.1 = (bf16[64,768]{1,0:T(8,128)(2,1)S(1)}, bf16[64,768]{1,0:T(8,128)(2,1)S(1)}, bf16[64,768]{1,0:T(8,128)(2,1)S(1)}, bf16[64,768]{1,0:T(8,128)(2,1)S(1)}, bf16[512,1536]{1,0:T(8,128)(2,1)S(1)}) custom-call(bf16[8,512]{1,0:T(8,128)(2,1)S(1)} %get-tuple-element.14.packet_ref.refs_0_, ...), custom_call_target="tpu_custom_call", output_to_operand_aliasing={{4}: (5, {})} | custom-call | flops 3221225472 | bytes 8388608 | tf_op jit(solution)/shard_map/named_rows/pallas_call | solution.py:381
  14.3 0.6 %collective-permute-start.3 = (bf16[64,768]{1,0:T(8,128)(2,1)S(1)}, bf16[64,768]{1,0:T(8,128)(2,1)S(1)}, u32[]{:S(2)}, u32[]{:S(2)}) collective-permute-start(bf16[64,768]{1,0:T(8,128)(2,1)S(1)} %get-tuple-element.22), channel_id=1, source_target_pairs={{0,1},{1,0},{2,3},{3,2},{4,5},{5,4},{6,7},{7,6},{8,9},{9,8},{10,11... | collective-permute-start | bytes 294920 | tf_op jit(solution)/shard_map/ppermute | solution.py:478
  14.9 0.5 %collective-permute-start.4 = (bf16[64,768]{1,0:T(8,128)(2,1)S(1)}, bf16[64,768]{1,0:T(8,128)(2,1)S(1)}, u32[]{:S(2)}, u32[]{:S(2)}) collective-permute-start(bf16[64,768]{1,0:T(8,128)(2,1)S(1)} %get-tuple-element.23), channel_id=1, source_target_pairs={{0,2},{1,3},{2,0},{3,1},{4,6},{5,7},{6,4},{7,5},{8,10},{9,11},{10,... | collective-permute-start | bytes 294920 | tf_op jit(solution)/shard_map/ppermute | solution.py:478
  15.4 2.4 %collective-permute-start.5 = (bf16[64,768]{1,0:T(8,128)(2,1)S(1)}, bf16[64,768]{1,0:T(8,128)(2,1)S(1)}, u32[]{:S(2)}, u32[]{:S(2)}) collective-permute-start(bf16[64,768]{1,0:T(8,128)(2,1)S(1)} %get-tuple-element.24), channel_id=1, source_target_pairs={{0,3},{1,2},{2,1},{3,0},{4,7},{5,6},{6,5},{7,4},{8,11},{9,10},{10,... | collective-permute-start | bytes 294920 | tf_op jit(solution)/shard_map/ppermute | solution.py:478
  17.8 5.1 %encode.1 = bf16[512,1536]{1,0:T(8,128)(2,1)} custom-call(bf16[512,1536]{1,0:T(8,128)(2,1)S(1)} %get-tuple-element.20.normed_ref, bf16[512,1536]{1,0:T(8,128)(2,1)S(1)} %copy-done.1, bf16[1536,1536]{1,0:T(8,128)(2,1)S(1)} %copy-done), custom_call_target="tpu_custom_call" | custom-call | flops 2415919104 | bytes 8388608 | tf_op jit(solution)/shard_map/encode/pallas_call | solution.py:428
  22.9 0.0 collective-permute-done.3.refs_1_
  23.0 0.0 collective-permute-done.4.refs_2_
  23.0 0.0 collective-permute-done.5.refs_3_
  23.0 1.0 %junction.1 = bf16[64,768]{1,0:T(8,128)(2,1)} custom-call(bf16[64,768]{1,0:T(8,128)(2,1)S(1)} %get-tuple-element.21.refs_0_, bf16[64,768]{1,0:T(8,128)(2,1)S(1)} %collective-permute-done.3.refs_1_, bf16[64,768]{1,0:T(8,128)(2,1)S(1)} %collective-permute-done.4.refs_2_, bf16[64,768]{1,0:T(8,128)(2,1)S(1)} %collective-permute-done.5.refs_3_, ...), custom_call_target="tpu_custom_call" | custom-call | tf_op jit(solution)/shard_map/junction/pallas_call | solution.py:464
  (1 shorter events, 0.0 us)
Async XLA Ops:
  1.3 5.7 %copy-start.4 = (f32[1536]{0:T(1024)S(1)}, f32[1536]{0:T(1024)}, u32[]{:S(2)}) copy-start(f32[1536]{0:T(1024)} %param.11) | copy-start | bytes 18436
  1.3 5.7 %copy-start = (bf16[1536,1536]{1,0:T(8,128)(2,1)S(1)}, bf16[1536,1536]{1,0:T(8,128)(2,1)}, u32[]{:S(2)}) copy-start(bf16[1536,1536]{1,0:T(8,128)(2,1)} %w_ref.3) | copy-start | bytes 14155780
  1.3 5.7 %copy-start.1 = (bf16[512,1536]{1,0:T(8,128)(2,1)S(1)}, bf16[512,1536]{1,0:T(8,128)(2,1)}, u32[]{:S(2)}) copy-start(bf16[512,1536]{1,0:T(8,128)(2,1)} %feat_ref.3) | copy-start | bytes 4718596
  1.3 5.7 %copy-start.2 = (bf16[1536,768]{1,0:T(8,128)(2,1)S(1)}, bf16[1536,768]{1,0:T(8,128)(2,1)}, u32[]{:S(2)}) copy-start(bf16[1536,768]{1,0:T(8,128)(2,1)} %refs_9_.1) | copy-start | bytes 7077892
  1.3 5.7 %copy-start.3 = (f32[5,1536]{1,0:T(8,128)S(1)}, f32[5,1536]{1,0:T(8,128)}, u32[]{:S(2)}) copy-start(f32[5,1536]{1,0:T(8,128)} %refs_6_.1) | copy-start | bytes 92164
  2.4 6.7 %collective-permute-start = (bf16[8,512]{1,0:T(8,128)(2,1)S(1)}, bf16[8,512]{1,0:T(8,128)(2,1)S(1)}, u32[]{:S(2)}, u32[]{:S(2)}) collective-permute-start(bf16[8,512]{1,0:T(8,128)(2,1)S(1)} %get-tuple-element.15), channel_id=1, source_target_pairs={{0,1},{1,0},{2,3},{3,2},{4,5},{5,4},{6,7},{7,6},{8,9},{9,8},{10,11... | collective-permute-start | bytes 24584 | tf_op jit(solution)/shard_map/ppermute | solution.py:478
  5.4 3.7 %collective-permute-start.1 = (bf16[8,512]{1,0:T(8,128)(2,1)S(1)}, bf16[8,512]{1,0:T(8,128)(2,1)S(1)}, u32[]{:S(2)}, u32[]{:S(2)}) collective-permute-start(bf16[8,512]{1,0:T(8,128)(2,1)S(1)} %get-tuple-element.16), channel_id=1, source_target_pairs={{0,2},{1,3},{2,0},{3,1},{4,6},{5,7},{6,4},{7,5},{8,10},{9,11},{10,... | collective-permute-start | bytes 24584 | tf_op jit(solution)/shard_map/ppermute | solution.py:478
  6.9 4.5 %collective-permute-start.2 = (bf16[8,512]{1,0:T(8,128)(2,1)S(1)}, bf16[8,512]{1,0:T(8,128)(2,1)S(1)}, u32[]{:S(2)}, u32[]{:S(2)}) collective-permute-start(bf16[8,512]{1,0:T(8,128)(2,1)S(1)} %get-tuple-element.17), channel_id=1, source_target_pairs={{0,3},{1,2},{2,1},{3,0},{4,7},{5,6},{6,5},{7,4},{8,11},{9,10},{10,... | collective-permute-start | bytes 24584 | tf_op jit(solution)/shard_map/ppermute | solution.py:478
  14.3 8.7 %collective-permute-start.3 = (bf16[64,768]{1,0:T(8,128)(2,1)S(1)}, bf16[64,768]{1,0:T(8,128)(2,1)S(1)}, u32[]{:S(2)}, u32[]{:S(2)}) collective-permute-start(bf16[64,768]{1,0:T(8,128)(2,1)S(1)} %get-tuple-element.22), channel_id=1, source_target_pairs={{0,1},{1,0},{2,3},{3,2},{4,5},{5,4},{6,7},{7,6},{8,9},{9,8},{10,11... | collective-permute-start | bytes 294920 | tf_op jit(solution)/shard_map/ppermute | solution.py:478
  14.9 8.1 %collective-permute-start.4 = (bf16[64,768]{1,0:T(8,128)(2,1)S(1)}, bf16[64,768]{1,0:T(8,128)(2,1)S(1)}, u32[]{:S(2)}, u32[]{:S(2)}) collective-permute-start(bf16[64,768]{1,0:T(8,128)(2,1)S(1)} %get-tuple-element.23), channel_id=1, source_target_pairs={{0,2},{1,3},{2,0},{3,1},{4,6},{5,7},{6,4},{7,5},{8,10},{9,11},{10,... | collective-permute-start | bytes 294920 | tf_op jit(solution)/shard_map/ppermute | solution.py:478
  15.4 7.6 %collective-permute-start.5 = (bf16[64,768]{1,0:T(8,128)(2,1)S(1)}, bf16[64,768]{1,0:T(8,128)(2,1)S(1)}, u32[]{:S(2)}, u32[]{:S(2)}) collective-permute-start(bf16[64,768]{1,0:T(8,128)(2,1)S(1)} %get-tuple-element.24), channel_id=1, source_target_pairs={{0,3},{1,2},{2,1},{3,0},{4,7},{5,6},{6,5},{7,4},{8,11},{9,10},{10,... | collective-permute-start | bytes 294920 | tf_op jit(solution)/shard_map/ppermute | solution.py:478

commit v4 on v3

--- a/solution.py
+++ b/solution.py
@@ -283,7 +283,8 @@
     ranks = jnp.dot(mine.astype(BF16), strict_upper(width), preferred_element_type=F32)
     sizes = jnp.sum(mine, axis=1, keepdims=True)
     total = jnp.sum(mine)
-    blocks = (total.astype(jnp.int32) + (block - 1)) // block
+    tail = block // 2
+    tails = (total.astype(jnp.int32) - block + (tail - 1)) // tail
     mark = F32(1 << 16)
     code = local + F32(1.0) + jnp.where(lane >= width // 2, mark, F32(0.0))
     offsets = []
@@ -324,15 +325,15 @@
         for j in range(columns):
             patched_ref[place : place + span, j * LANES : (j + 1) * LANES] = out[j]
 
-    spread = lax.broadcasted_iota(jnp.int32, (block, rows), 1).astype(F32)
-    level = lax.broadcasted_iota(jnp.int32, (block, width), 0).astype(F32)
-    slot = lax.broadcasted_iota(jnp.int32, (capacity, block), 0).astype(F32)
-    column = lax.broadcasted_iota(jnp.int32, (capacity, block), 1).astype(F32)
     wide = 256
 
-    def encode_block(c, store):
-        base = F32(c * block) if isinstance(c, int) else (c * block).astype(F32)
-        found = jnp.zeros((block, width), F32)
+    def encode_block(base, size, store):
+        spread = lax.broadcasted_iota(jnp.int32, (size, rows), 1).astype(F32)
+        level = lax.broadcasted_iota(jnp.int32, (size, width), 0).astype(F32)
+        slot = lax.broadcasted_iota(jnp.int32, (capacity, size), 0).astype(F32)
+        column = lax.broadcasted_iota(jnp.int32, (capacity, size), 1).astype(F32)
+        part = slice(0, size)
+        found = jnp.zeros((size, width), F32)
         for k in range(owners):
             found = jnp.where(spots[k] - base == level, code[k : k + 1, :], found)
         found = jnp.sum(found, axis=1, keepdims=True)
@@ -341,22 +342,21 @@
         grab = jnp.where(spread == index, F32(1.0), F32(0.0)).astype(BF16)
         for j in range(channels // wide):
             lanes = slice(j * wide, (j + 1) * wide)
-            lhs[:, lanes] = jnp.dot(grab, patched_ref[:, lanes], preferred_element_type=F32).astype(BF16)
-            res[:, lanes] = jnp.dot(grab, feat_ref[:, lanes], preferred_element_type=F32).astype(BF16)
+            lhs[part, lanes] = jnp.dot(grab, patched_ref[:, lanes], preferred_element_type=F32).astype(BF16)
+            res[part, lanes] = jnp.dot(grab, feat_ref[:, lanes], preferred_element_type=F32).astype(BF16)
         for j in range(channels // wide):
             lanes = slice(j * wide, (j + 1) * wide)
-            mixed = jnp.dot(lhs[...], w_ref[:, lanes], preferred_element_type=F32)
-            enc[:, lanes] = (res[:, lanes].astype(F32) + gelu(mixed)).astype(BF16)
+            mixed = jnp.dot(lhs[part, :], w_ref[:, lanes], preferred_element_type=F32)
+            enc[part, lanes] = (res[part, lanes].astype(F32) + gelu(mixed)).astype(BF16)
         for j in range(heads // wide):
             lanes = slice(j * wide, (j + 1) * wide)
-            left = jnp.dot(enc[...], wd_ref[:, lanes], preferred_element_type=F32)
-            right = jnp.dot(enc[...], wa_ref[:, lanes], preferred_element_type=F32)
-            proj[:, lanes] = jnp.where(accepts, right, left).astype(BF16)
+            left = jnp.dot(enc[part, :], wd_ref[:, lanes], preferred_element_type=F32)
+            right = jnp.dot(enc[part, :], wa_ref[:, lanes], preferred_element_type=F32)
+            proj[part, lanes] = jnp.where(accepts, right, left).astype(BF16)
         for k in range(owners):
             put = (column + base == offsets[k] + slot) & (slot < sizes[k : k + 1])
             put = jnp.where(put, F32(1.0), F32(0.0)).astype(BF16)
-            placed = jnp.dot(put, proj[...], preferred_element_type=F32)
-            store(outs[k], placed)
+            store(outs[k], jnp.dot(put, proj[part, :], preferred_element_type=F32))
 
     def write(ref, value):
         ref[...] = value.astype(BF16)
@@ -364,13 +364,13 @@
     def add(ref, value):
         ref[...] = (ref[...].astype(F32) + value).astype(BF16)
 
-    encode_block(0, write)
+    encode_block(F32(0.0), block, write)
 
     def body(c, carry):
-        encode_block(c, add)
+        encode_block((block + c * tail).astype(F32), tail, add)
         return carry
 
-    lax.fori_loop(1, blocks, body, 0)
+    lax.fori_loop(0, tails, body, 0)
 
 
 def named(packets, feat, normed, taps, gain, w, wd, wa, width, capacity):
@@ -441,21 +441,27 @@
 
 def junction_kernel(owners, *refs):
     blocks = refs[:owners]
-    spread_ref, out_ref = refs[owners:]
-    slots = out_ref.shape[0]
-    capacity = blocks[0].shape[0]
-    picked = None
-    for k in range(owners):
-        part = lax.dot_general(
-            spread_ref[k * capacity : (k + 1) * capacity, :],
-            blocks[k][...],
+    spread_ref, out_hbm, stage, sem = refs[owners:]
+    slots, heads = out_hbm.shape
+    wide = 256
+    copies = []
+    for j in range(heads // wide):
+        lanes = slice(j * wide, (j + 1) * wide)
+        picked = lax.dot_general(
+            spread_ref[...],
+            jnp.concatenate([block[:, lanes] for block in blocks], axis=0),
             (((0,), (0,)), ((), ())),
             preferred_element_type=F32,
         )
-        picked = part if picked is None else picked + part
-    left, right = picked[:slots], picked[slots:]
-    silu = left / (F32(1.0) + jnp.exp(-left))
-    out_ref[...] = (silu * right).astype(BF16)
+        left, right = picked[:slots], picked[slots:]
+        silu = left / (F32(1.0) + jnp.exp(-left))
+        stage[:, lanes] = (silu * right).astype(BF16)
+        at = pl.ds(j * wide, wide)
+        copy = pltpu.make_async_copy(stage.at[:, at], out_hbm.at[:, at], sem.at[j])
+        copy.start()
+        copies.append(copy)
+    for copy in copies:
+        copy.wait()
 
 
 def junction(blocks, spread):
@@ -464,8 +470,9 @@
     return pl.pallas_call(
         functools.partial(junction_kernel, len(blocks)),
         in_specs=[whole()] * (len(blocks) + 1),
-        out_specs=whole(),
+        out_specs=in_hbm(),
         out_shape=jax.ShapeDtypeStruct((slots, heads), BF16),
+        scratch_shapes=[pltpu.VMEM((slots, heads), BF16), pltpu.SemaphoreType.DMA((heads // 256,))],
         compiler_params=params(6),
         name="junction",
     )(*blocks, spread)

time: 24.2 us -> 24 us (level)
  no operation moved by 1% of the time
where the time goes in v4:
time: 24 us; the launch traced here: 23.9 us
  Pallas kernels  11.9 us (50%)
  starting transfers between devices  8.13 us (34%)
  waiting for transfers between devices  2.45 us (10%)
  between operations  1.42 us (6%)
    ppermute x6, starting transfers between devices, swap_all(): lax.ppermute(arrays[k], 'seq', [(i, i ^ k) for i in range(owners)])  8.13 us
    pallas_call x1, Pallas kernels, encode(): pl.pallas_call(encode_kernel, in_specs=[whole()] * 3, out_specs=pl.BlockS...  5.14 us
    pallas_call x1, Pallas kernels, named(): pl.pallas_call(functools.partial(named_kernel, owners, capacity, width),...  2.78 us
    ppermute x6, waiting for transfers between devices, swap_all(): lax.ppermute(arrays[k], 'seq', [(i, i ^ k) for i in range(owners)])  2.45 us
    pallas_call x1, Pallas kernels, conv_norm(): pl.pallas_call(functools.partial(conv_kernel, owners, capacity, width), i...  2.02 us
    pallas_call x1, Pallas kernels, pack(): pl.pallas_call(functools.partial(pack_kernel, owners), in_specs=[in_hbm()...  1.03 us
    pallas_call x1, Pallas kernels, junction(): pl.pallas_call(functools.partial(junction_kernel, len(blocks)), in_specs=...  0.9 us
  transfers between devices with their start and end apart: 6, of which 1 were waited for; matrix products, arithmetic and copies ran while one was open for 0% of the time, Pallas kernels for 30%

profile of v4, /device:TPU:0, one launch (start us, length us, event | category | flops | bytes accessed | tf_op | source)
XLA Modules:
  0.0 23.9 jit_solution(2094911079766009662)
XLA Ops:
  1.3 0.0 copy-start.4
  1.3 0.0 copy-start
  1.3 0.0 copy-start.1
  1.3 0.0 copy-start.2
  1.3 0.0 copy-start.3
  1.3 1.0 %pack.1 = (bf16[8,512]{1,0:T(8,128)(2,1)S(1)}, bf16[8,512]{1,0:T(8,128)(2,1)S(1)}, bf16[8,512]{1,0:T(8,128)(2,1)S(1)}, bf16[8,512]{1,0:T(8,128)(2,1)S(1)}) custom-call(bf16[512,1536]{1,0:T(8,128)(2,1)} %feat_ref.3, s32[1,64]{1,0:T(1,128)} %bitcast.2, s32[1,64]{1,0:T(1,128)} %bitcast.3, s32[1]{0:T(128)S(6)} %copy.13.count), custom_call_target="tpu_custom_call" | custom-call | flops 15728640000 | bytes 1048576 | tf_op jit(solution)/shard_map/pack/pallas_call | solution.py:93
  2.4 3.0 %collective-permute-start = (bf16[8,512]{1,0:T(8,128)(2,1)S(1)}, bf16[8,512]{1,0:T(8,128)(2,1)S(1)}, u32[]{:S(2)}, u32[]{:S(2)}) collective-permute-start(bf16[8,512]{1,0:T(8,128)(2,1)S(1)} %get-tuple-element.15), channel_id=1, source_target_pairs={{0,1},{1,0},{2,3},{3,2},{4,5},{5,4},{6,7},{7,6},{8,9},{9,8},{10,11... | collective-permute-start | bytes 24584 | tf_op jit(solution)/shard_map/ppermute | solution.py:485
  5.4 1.5 %collective-permute-start.1 = (bf16[8,512]{1,0:T(8,128)(2,1)S(1)}, bf16[8,512]{1,0:T(8,128)(2,1)S(1)}, u32[]{:S(2)}, u32[]{:S(2)}) collective-permute-start(bf16[8,512]{1,0:T(8,128)(2,1)S(1)} %get-tuple-element.16), channel_id=1, source_target_pairs={{0,2},{1,3},{2,0},{3,1},{4,6},{5,7},{6,4},{7,5},{8,10},{9,11},{10,... | collective-permute-start | bytes 24584 | tf_op jit(solution)/shard_map/ppermute | solution.py:485
  6.9 0.0 collective-permute-start.2
  6.9 0.0 copy-done.4
  7.0 0.0 copy-done
  7.0 0.0 copy-done.1
  7.0 0.0 copy-done.2
  7.0 0.0 copy-done.3
  7.0 2.0 %conv_norm.1 = (bf16[512,1536]{1,0:T(8,128)(2,1)S(1)}, bf16[1536,768]{1,0:T(8,128)(2,1)S(1)}, bf16[256,128]{1,0:T(8,128)(2,1)S(1)}) custom-call(bf16[8,512]{1,0:T(8,128)(2,1)S(1)} %get-tuple-element.14.packet_ref.refs_0_, bf16[512,1536]{1,0:T(8,128)(2,1)S(1)} %copy-done.1, f32[5,1536]{1,0:T(8,128)S(1)} %copy-done.3, f32[1,1536]{1,0:T(1,128)S(1)} %reshape.16.gain_ref.refs_7_, ...), custom_call_target="tpu_custom_call" | custom-call | flops 15728640000 | bytes 12582912 | tf_op jit(solution)/shard_map/conv_norm/pallas_call | solution.py:237
  9.0 0.0 collective-permute-done.refs_1_
  9.0 0.0 collective-permute-done.1.refs_2_
  9.1 2.4 %collective-permute-done.2.refs_3_ = bf16[8,512]{1,0:T(8,128)(2,1)S(1)} collective-permute-done((bf16[8,512]{1,0:T(8,128)(2,1)S(1)}, bf16[8,512]{1,0:T(8,128)(2,1)S(1)}, u32[]{:S(2)}, u32[]{:S(2)}) %collective-permute-start.2) | collective-permute-done | bytes 8224 | tf_op jit(solution)/shard_map/ppermute | solution.py:485
  11.5 2.8 %named_rows.1 = (bf16[64,768]{1,0:T(8,128)(2,1)S(1)}, bf16[64,768]{1,0:T(8,128)(2,1)S(1)}, bf16[64,768]{1,0:T(8,128)(2,1)S(1)}, bf16[64,768]{1,0:T(8,128)(2,1)S(1)}, bf16[512,1536]{1,0:T(8,128)(2,1)S(1)}) custom-call(bf16[8,512]{1,0:T(8,128)(2,1)S(1)} %get-tuple-element.14.packet_ref.refs_0_, ...), custom_call_target="tpu_custom_call", output_to_operand_aliasing={{4}: (5, {})} | custom-call | flops 3221225472 | bytes 8388608 | tf_op jit(solution)/shard_map/named_rows/pallas_call | solution.py:381
  14.3 0.6 %collective-permute-start.3 = (bf16[64,768]{1,0:T(8,128)(2,1)S(1)}, bf16[64,768]{1,0:T(8,128)(2,1)S(1)}, u32[]{:S(2)}, u32[]{:S(2)}) collective-permute-start(bf16[64,768]{1,0:T(8,128)(2,1)S(1)} %get-tuple-element.22), channel_id=1, source_target_pairs={{0,1},{1,0},{2,3},{3,2},{4,5},{5,4},{6,7},{7,6},{8,9},{9,8},{10,11... | collective-permute-start | bytes 294920 | tf_op jit(solution)/shard_map/ppermute | solution.py:485
  14.9 0.5 %collective-permute-start.4 = (bf16[64,768]{1,0:T(8,128)(2,1)S(1)}, bf16[64,768]{1,0:T(8,128)(2,1)S(1)}, u32[]{:S(2)}, u32[]{:S(2)}) collective-permute-start(bf16[64,768]{1,0:T(8,128)(2,1)S(1)} %get-tuple-element.23), channel_id=1, source_target_pairs={{0,2},{1,3},{2,0},{3,1},{4,6},{5,7},{6,4},{7,5},{8,10},{9,11},{10,... | collective-permute-start | bytes 294920 | tf_op jit(solution)/shard_map/ppermute | solution.py:485
  15.4 2.4 %collective-permute-start.5 = (bf16[64,768]{1,0:T(8,128)(2,1)S(1)}, bf16[64,768]{1,0:T(8,128)(2,1)S(1)}, u32[]{:S(2)}, u32[]{:S(2)}) collective-permute-start(bf16[64,768]{1,0:T(8,128)(2,1)S(1)} %get-tuple-element.24), channel_id=1, source_target_pairs={{0,3},{1,2},{2,1},{3,0},{4,7},{5,6},{6,5},{7,4},{8,11},{9,10},{10,... | collective-permute-start | bytes 294920 | tf_op jit(solution)/shard_map/ppermute | solution.py:485
  17.8 5.1 %encode.1 = bf16[512,1536]{1,0:T(8,128)(2,1)} custom-call(bf16[512,1536]{1,0:T(8,128)(2,1)S(1)} %get-tuple-element.20.normed_ref, bf16[512,1536]{1,0:T(8,128)(2,1)S(1)} %copy-done.1, bf16[1536,1536]{1,0:T(8,128)(2,1)S(1)} %copy-done), custom_call_target="tpu_custom_call" | custom-call | flops 2415919104 | bytes 8388608 | tf_op jit(solution)/shard_map/encode/pallas_call | solution.py:428
  23.0 0.0 collective-permute-done.3.refs_1_
  23.0 0.0 collective-permute-done.4.refs_2_
  23.0 0.0 collective-permute-done.5.refs_3_
  23.0 0.9 %junction.1 = bf16[64,768]{1,0:T(8,128)(2,1)} custom-call(bf16[64,768]{1,0:T(8,128)(2,1)S(1)} %get-tuple-element.21.refs_0_, bf16[64,768]{1,0:T(8,128)(2,1)S(1)} %collective-permute-done.3.refs_1_, bf16[64,768]{1,0:T(8,128)(2,1)S(1)} %collective-permute-done.4.refs_2_, bf16[64,768]{1,0:T(8,128)(2,1)S(1)} %collective-permute-done.5.refs_3_, ...), custom_call_target="tpu_custom_call" | custom-call | tf_op jit(solution)/shard_map/junction/pallas_call | solution.py:470
  (1 shorter events, 0.0 us)
Async XLA Ops:
  1.3 5.7 %copy-start.4 = (f32[1536]{0:T(1024)S(1)}, f32[1536]{0:T(1024)}, u32[]{:S(2)}) copy-start(f32[1536]{0:T(1024)} %param.11) | copy-start | bytes 18436
  1.3 5.7 %copy-start = (bf16[1536,1536]{1,0:T(8,128)(2,1)S(1)}, bf16[1536,1536]{1,0:T(8,128)(2,1)}, u32[]{:S(2)}) copy-start(bf16[1536,1536]{1,0:T(8,128)(2,1)} %w_ref.3) | copy-start | bytes 14155780
  1.3 5.7 %copy-start.1 = (bf16[512,1536]{1,0:T(8,128)(2,1)S(1)}, bf16[512,1536]{1,0:T(8,128)(2,1)}, u32[]{:S(2)}) copy-start(bf16[512,1536]{1,0:T(8,128)(2,1)} %feat_ref.3) | copy-start | bytes 4718596
  1.3 5.7 %copy-start.2 = (bf16[1536,768]{1,0:T(8,128)(2,1)S(1)}, bf16[1536,768]{1,0:T(8,128)(2,1)}, u32[]{:S(2)}) copy-start(bf16[1536,768]{1,0:T(8,128)(2,1)} %refs_9_.1) | copy-start | bytes 7077892
  1.3 5.7 %copy-start.3 = (f32[5,1536]{1,0:T(8,128)S(1)}, f32[5,1536]{1,0:T(8,128)}, u32[]{:S(2)}) copy-start(f32[5,1536]{1,0:T(8,128)} %refs_6_.1) | copy-start | bytes 92164
  2.4 6.7 %collective-permute-start = (bf16[8,512]{1,0:T(8,128)(2,1)S(1)}, bf16[8,512]{1,0:T(8,128)(2,1)S(1)}, u32[]{:S(2)}, u32[]{:S(2)}) collective-permute-start(bf16[8,512]{1,0:T(8,128)(2,1)S(1)} %get-tuple-element.15), channel_id=1, source_target_pairs={{0,1},{1,0},{2,3},{3,2},{4,5},{5,4},{6,7},{7,6},{8,9},{9,8},{10,11... | collective-permute-start | bytes 24584 | tf_op jit(solution)/shard_map/ppermute | solution.py:485
  5.4 3.7 %collective-permute-start.1 = (bf16[8,512]{1,0:T(8,128)(2,1)S(1)}, bf16[8,512]{1,0:T(8,128)(2,1)S(1)}, u32[]{:S(2)}, u32[]{:S(2)}) collective-permute-start(bf16[8,512]{1,0:T(8,128)(2,1)S(1)} %get-tuple-element.16), channel_id=1, source_target_pairs={{0,2},{1,3},{2,0},{3,1},{4,6},{5,7},{6,4},{7,5},{8,10},{9,11},{10,... | collective-permute-start | bytes 24584 | tf_op jit(solution)/shard_map/ppermute | solution.py:485
  6.9 4.5 %collective-permute-start.2 = (bf16[8,512]{1,0:T(8,128)(2,1)S(1)}, bf16[8,512]{1,0:T(8,128)(2,1)S(1)}, u32[]{:S(2)}, u32[]{:S(2)}) collective-permute-start(bf16[8,512]{1,0:T(8,128)(2,1)S(1)} %get-tuple-element.17), channel_id=1, source_target_pairs={{0,3},{1,2},{2,1},{3,0},{4,7},{5,6},{6,5},{7,4},{8,11},{9,10},{10,... | collective-permute-start | bytes 24584 | tf_op jit(solution)/shard_map/ppermute | solution.py:485
  14.3 8.7 %collective-permute-start.3 = (bf16[64,768]{1,0:T(8,128)(2,1)S(1)}, bf16[64,768]{1,0:T(8,128)(2,1)S(1)}, u32[]{:S(2)}, u32[]{:S(2)}) collective-permute-start(bf16[64,768]{1,0:T(8,128)(2,1)S(1)} %get-tuple-element.22), channel_id=1, source_target_pairs={{0,1},{1,0},{2,3},{3,2},{4,5},{5,4},{6,7},{7,6},{8,9},{9,8},{10,11... | collective-permute-start | bytes 294920 | tf_op jit(solution)/shard_map/ppermute | solution.py:485
  14.9 8.1 %collective-permute-start.4 = (bf16[64,768]{1,0:T(8,128)(2,1)S(1)}, bf16[64,768]{1,0:T(8,128)(2,1)S(1)}, u32[]{:S(2)}, u32[]{:S(2)}) collective-permute-start(bf16[64,768]{1,0:T(8,128)(2,1)S(1)} %get-tuple-element.23), channel_id=1, source_target_pairs={{0,2},{1,3},{2,0},{3,1},{4,6},{5,7},{6,4},{7,5},{8,10},{9,11},{10,... | collective-permute-start | bytes 294920 | tf_op jit(solution)/shard_map/ppermute | solution.py:485
  15.4 7.6 %collective-permute-start.5 = (bf16[64,768]{1,0:T(8,128)(2,1)S(1)}, bf16[64,768]{1,0:T(8,128)(2,1)S(1)}, u32[]{:S(2)}, u32[]{:S(2)}) collective-permute-start(bf16[64,768]{1,0:T(8,128)(2,1)S(1)} %get-tuple-element.24), channel_id=1, source_target_pairs={{0,3},{1,2},{2,1},{3,0},{4,7},{5,6},{6,5},{7,4},{8,11},{9,10},{10,... | collective-permute-start | bytes 294920 | tf_op jit(solution)/shard_map/ppermute | solution.py:485
